TPU v7x, 256 devices: a whole 4x4x8 slice. The times are simulated.
256 devices in a mesh: ia: 4 (over y), ja: 8 (over x, core), ka: 8 (over z).
Axes of the slice: x: 4, y: 4, z: 8, core: 2. Of those that a mesh axis runs over, the one named last changes fastest.
Arguments:
- observed: bfloat16 [4, 8, 40, 128, 32, 128], P('ia', 'ja', 'ka'), may hold values from -6 to 6
- weights: bfloat16 [4, 8, 40, 128, 32, 128], P('ia', 'ja', 'ka'), may hold values from 0 to 4, as said below
- coords: int32 [4, 8, 40, 3], P('ia', 'ja', 'ka'), may hold values from 0 to 31, as said below
- counts: int32 [4, 8, 8], P('ia', 'ja', 'ka'), may hold values from 0 to 5, as said below
- factor_rows: bfloat16 [64, 4096], P(None, ('ia', 'ja', 'ka')), may hold values from -0.75 to 0.75
- factor_cols: bfloat16 [64, 4096], P(None, ('ja', 'ka')), may hold values from -0.75 to 0.75
- factor_depth: bfloat16 [64, 1024], replicated, may hold values from -0.75 to 0.75
- core_tensor: bfloat16 [64, 64, 64], replicated, may hold values from -6 to 6
Outputs:
- rows_gradient: float32 [64, 4096], P(None, ('ia', 'ja', 'ka'))
- cols_gradient: float32 [64, 4096], P(None, ('ja', 'ka'))
- depth_gradient: float32 [64, 1024], P(None, 'ka')
- core_gradient: float32 [64, 64, 64], replicated
Inputs may be any that keep to these rules, and one draw needn't show every extreme that they name: counts[a, b, c] is the number of live slots of the device at index a of ia, b of ja, c of ka; the busiest devices hold 5. coords[a, b, c * 5 + s] = (p, q, t) with a * 8 <= p < (a + 1) * 8, b * 4 <= q < (b + 1) * 4, c * 4 <= t < (c + 1) * 4; the 5 slots of one device name distinct blocks. `weights`: zero at unobserved entries, positive at observed ones.
All inputs are finite; a program needn't handle non-finite values.
Results may differ from a plain program's by a relative error of at most 0.0012.
Values may be sent and summed in bfloat16 or wider, within the bound.
A program may use at most 64 MiB of HBM per device.

v0:
```python
import jax
import jax.numpy as jnp
from jax import lax
from jax.sharding import PartitionSpec as P

resid_scale = 1.0 / 64.0


def block_terms(observed_block, weight_block, row_factor, col_factor, depth_factor, core_tensor):
    rank_width, block_rows = row_factor.shape
    block_cols = col_factor.shape[1]
    slab_depth = depth_factor.shape[1]
    core_flat = core_tensor.reshape(rank_width * rank_width, rank_width)
    first_cube = jnp.dot(core_flat, depth_factor, preferred_element_type=jnp.float32).astype(
        jnp.bfloat16
    )
    first_cube = first_cube.reshape(rank_width, rank_width, slab_depth)
    second_cube = jnp.einsum(
        "rsk,sj->rkj", first_cube, col_factor, preferred_element_type=jnp.float32
    ).astype(jnp.bfloat16)
    second_flat = second_cube.reshape(rank_width, slab_depth * block_cols)
    model_block = lax.dot_general(
        row_factor, second_flat, (((0,), (0,)), ((), ())), preferred_element_type=jnp.float32
    )
    weight_flat = weight_block.reshape(block_rows, slab_depth * block_cols).astype(jnp.float32)
    data_flat = observed_block.reshape(block_rows, slab_depth * block_cols).astype(jnp.float32)
    residual = (weight_flat * (model_block - data_flat) * resid_scale).astype(jnp.bfloat16)
    row_term = lax.dot_general(
        second_flat, residual, (((1,), (1,)), ((), ())), preferred_element_type=jnp.float32
    )
    first_back = jnp.dot(row_factor, residual, preferred_element_type=jnp.float32).astype(
        jnp.bfloat16
    )
    back_cube = first_back.reshape(rank_width, slab_depth, block_cols)
    col_term = jnp.einsum("rsk,rkj->sj", first_cube, back_cube, preferred_element_type=jnp.float32)
    second_back = jnp.einsum(
        "sj,rkj->rsk", col_factor, back_cube, preferred_element_type=jnp.float32
    ).astype(jnp.bfloat16)
    back_flat = second_back.reshape(rank_width * rank_width, slab_depth)
    depth_term = lax.dot_general(
        core_flat, back_flat, (((0,), (0,)), ((), ())), preferred_element_type=jnp.float32
    )
    core_term = lax.dot_general(
        back_flat, depth_factor, (((1,), (1,)), ((), ())), preferred_element_type=jnp.float32
    )
    return (row_term, col_term, depth_term, core_term.reshape(rank_width, rank_width, rank_width))


def add_columns(table, piece, start_col):
    width = piece.shape[1]
    return lax.dynamic_update_slice_in_dim(
        table, lax.dynamic_slice_in_dim(table, start_col, width, 1) + piece, start_col, 1
    )


def accumulate_blocks(
    live_count,
    data_slots,
    weight_slots,
    coord_slots,
    row_table,
    col_table,
    factor_depth,
    core_tensor,
    row_base,
    col_base,
):
    rank_width = core_tensor.shape[0]
    block_rows = data_slots.shape[1]
    slab_depth = data_slots.shape[2]
    block_cols = data_slots.shape[3]
    start_sums = (
        jnp.zeros((rank_width, row_table.shape[1]), jnp.float32),
        jnp.zeros((rank_width, col_table.shape[1]), jnp.float32),
        jnp.zeros((rank_width, factor_depth.shape[1]), jnp.float32),
        jnp.zeros((rank_width, rank_width, rank_width), jnp.float32),
    )

    def add_slot(slot_index, running):
        rows_sum, cols_sum, depth_sum, core_sum = running
        position = coord_slots[slot_index]
        row_start = (position[0] - row_base) * block_rows
        col_start = (position[1] - col_base) * block_cols
        depth_start = position[2] * slab_depth
        row_factor = lax.dynamic_slice_in_dim(row_table, row_start, block_rows, 1)
        col_factor = lax.dynamic_slice_in_dim(col_table, col_start, block_cols, 1)
        depth_factor = lax.dynamic_slice_in_dim(factor_depth, depth_start, slab_depth, 1)
        block_sums = block_terms(
            data_slots[slot_index],
            weight_slots[slot_index],
            row_factor,
            col_factor,
            depth_factor,
            core_tensor,
        )
        rows_sum = add_columns(rows_sum, block_sums[0], row_start)
        cols_sum = add_columns(cols_sum, block_sums[1], col_start)
        depth_sum = add_columns(depth_sum, block_sums[2], depth_start)
        return (rows_sum, cols_sum, depth_sum, core_sum + block_sums[3])

    return lax.fori_loop(0, live_count, add_slot, start_sums)


def on_device(
    observed, weights, coords, counts, factor_rows, factor_cols, factor_depth, core_tensor
):
    slot_count = observed.shape[2]
    data_slots = observed.reshape(observed.shape[2:])
    weight_slots = weights.reshape(weights.shape[2:])
    coord_slots = coords.reshape(slot_count, 3)
    own_count = counts.reshape(())
    row_table = lax.all_gather(factor_rows, ("ja", "ka"), axis=1, tiled=True)
    col_table = lax.all_gather(factor_cols, "ka", axis=1, tiled=True)
    row_base = lax.axis_index("ia") * (row_table.shape[1] // observed.shape[3])
    col_base = lax.axis_index("ja") * (col_table.shape[1] // observed.shape[5])
    rows_sum, cols_sum, depth_sum, core_sum = accumulate_blocks(
        own_count,
        data_slots,
        weight_slots,
        coord_slots,
        row_table,
        col_table,
        factor_depth,
        core_tensor,
        row_base,
        col_base,
    )
    rows_gradient = lax.psum_scatter(rows_sum, ("ja", "ka"), scatter_dimension=1, tiled=True)
    cols_whole = lax.psum(cols_sum, "ia")
    depth_whole = lax.psum(depth_sum, ("ia", "ja"))
    cols_gradient, depth_gradient = (
        lax.psum_scatter(cols_whole, "ka", scatter_dimension=1, tiled=True),
        lax.psum_scatter(depth_whole, "ka", scatter_dimension=1, tiled=True),
    )
    core_gradient = lax.psum(core_sum, ("ia", "ja", "ka"))
    return (rows_gradient, cols_gradient, depth_gradient, core_gradient)


def solution(mesh):
    in_specs = (
        P("ia", "ja", "ka", None, None, None),
        P("ia", "ja", "ka", None, None, None),
        P("ia", "ja", "ka", None),
        P("ia", "ja", "ka"),
        P(None, ("ia", "ja", "ka")),
        P(None, ("ja", "ka")),
        P(),
        P(),
    )
    out_specs = (P(None, ("ia", "ja", "ka")), P(None, ("ja", "ka")), P(None, "ka"), P())
    return jax.shard_map(
        on_device, mesh=mesh, in_specs=in_specs, out_specs=out_specs, check_vma=False
    )
```

profile of v0, /device:TPU:1, one launch (start us, length us, event | category | flops | bytes accessed | tf_op | source)
XLA Modules:
  0.0 614.4 jit_solution(5447334796632463020)
XLA Ops:
  8.0 48.0 %all_gather.7 = bf16[64,1024]{0,1:T(8,128)(2,1)S(1)} all-gather(bf16[64,16]{0,1:T(8,128)(2,1)} %param.14), channel_id=1, replica_groups=mesh['ia'=4,'ja'=8,'ka'=8] {'ja','ka'}, dimensions={1}, use_global_device_ids=true | all-gather | bytes 133120 | tf_op jit(solution)/shard_map/all_gather | solution.py:112
  56.1 0.1 copy.27
  56.2 1.1 copy.25
  57.3 0.8 copy.23
  58.1 18.2 %all_gather.6 = bf16[64,512]{0,1:T(8,128)(2,1)S(1)} all-gather(bf16[64,64]{0,1:T(8,128)(2,1)S(1)} %copy.23), channel_id=1, replica_groups=mesh['ia'=4,'ja'=8,'ka'=8] {'ka'}, dimensions={1}, use_global_device_ids=true | all-gather | bytes 73728 | tf_op jit(solution)/shard_map/all_gather | solution.py:113
  76.5 0.7 copy.56
  77.1 1.6 broadcast_in_dim.7
  78.8 28.4 %while.16 = (s32[]{:T(128)}, f32[64,1024]{1,0:T(8,128)S(1)}, f32[64,512]{1,0:T(8,128)S(1)}, f32[64,1024]{0,1:T(8,128)S(1)}, f32[64,64,64]{2,1,0:T(8,128)}, /*ind...) while((s32[]{:T(128)}, f32[64,1024]{1,0:T(8,128)S(1)}, ...), condition=%wide.region_1.0_spmd, body=%wide.region_0.0_spmd.sunk | while | flops 356534272 | bytes 34849308 | solution.py:101
  79.6 0.6 fusion.87
  80.8 0.4 fusion.88
  81.2 0.6 reshape.62
  82.4 0.4 convolution_convert_fusion.6
  83.5 2.1 dynamic-slice_convert_fusion.3
  85.6 2.7 fusion.89
  88.3 0.3 convolution_convert_fusion.7
  88.7 0.3 fusion.92
  89.0 0.9 copy-done.1
  89.9 0.7 convolution_add_fusion.3
  90.6 0.3 fusion.93
  90.9 1.0 copy-done.2
  91.9 0.3 fusion.91
  92.2 0.5 fusion.90
  93.4 0.6 fusion.87
  94.6 0.4 fusion.88
  95.1 0.6 reshape.62
  96.3 0.4 convolution_convert_fusion.6
  97.4 2.1 dynamic-slice_convert_fusion.3
  99.5 2.7 fusion.89
  102.2 0.3 convolution_convert_fusion.7
  102.6 0.3 fusion.92
  102.9 0.9 copy-done.1
  103.8 0.7 convolution_add_fusion.3
  104.4 0.3 fusion.93
  104.8 1.0 copy-done.2
  105.8 0.3 fusion.91
  106.1 0.5 fusion.90
  107.2 1.0 copy.28
  108.3 0.8 copy.31
  109.2 0.9 copy.29
  110.2 0.7 all-reduce.4.cloned.1.call-update
  110.9 0.6 dynamic-slice
  112.1 223.5 %all-reduce.6.cloned.1.call-done = f32[64,1024]{0,1:T(8,128)} async-done(((f32[64,1024]{0,1:T(8,128)}), f32[64,1024]{0,1:T(8,128)}) %all-reduce.6.cloned.1.call-update) | async-done | bytes 262160
  335.7 1.3 constant_dynamic-slice_fusion.1
  336.9 0.8 copy.32
  337.8 13.9 %psum.24 = f32[64,64]{1,0:T(8,128)} all-reduce(f32[64,64]{1,0:T(8,128)S(1)} %copy.32), channel_id=1, replica_groups=mesh['ia'=4,'ja'=8,'ka'=8] {'ia'}, use_global_device_ids=true, to_apply=%region_3.0 | all-reduce | flops 4096 | bytes 32768 | tf_op jit(solution)/shard_map/psum | solution.py:129
  351.7 124.8 %psum.25 = f32[64,128]{1,0:T(8,128)} all-reduce(f32[64,128]{1,0:T(8,128)} %reduce-scatter.5.cloned.1.call-done), channel_id=1, replica_groups=mesh['ia'=4,'ja'=8,'ka'=8] {'ia','ja'}, use_global_device_ids=true, to_apply=%region_5.0 | all-reduce | flops 8192 | bytes 65536 | tf_op jit(solution)/shard_map/psum | solution.py:130
  476.5 127.3 %all-reduce.4.cloned.1.call-done = f32[64,64,64]{2,1,0:T(8,128)} async-done(((f32[64,64,64]{2,1,0:T(8,128)}), f32[64,64,64]{2,1,0:T(8,128)}) %all-reduce.4.cloned.1.call-update) | async-done | bytes 1048592 | tf_op jit(solution)/shard_map/psum | solution.py:135
  603.8 3.2 copy.91
  (25 shorter events, 0.7 us)
Async XLA Ops:
  8.0 327.7 %all-reduce.6.cloned.1.call-start = ((), (), s32[]{:S(2)}) async-start(), calls=%async_computation.5 | async-start | bytes 1048576
  56.1 22.8 %copy-start = (bf16[64,64,64]{2,1,0:T(8,128)(2,1)S(1)}, bf16[64,64,64]{2,1,0:T(8,128)(2,1)}, u32[]{:S(2)}) copy-start(bf16[64,64,64]{2,1,0:T(8,128)(2,1)} %param.17) | copy-start | bytes 1572868
  88.3 1.6 copy-start.1
  90.6 1.3 copy-start.2
  102.2 1.6 copy-start.1
  104.4 1.3 copy-start.2
  108.2 2.7 copy-start.3
  108.3 228.7 %reduce-scatter.7.cloned.1.call-start = ((), (), s32[]{:S(2)}) async-start(), calls=%async_computation.4 | async-start | bytes 294912
  109.2 242.5 %reduce-scatter.5.cloned.1.call-start = ((), (), s32[]{:S(2)}) async-start(), calls=%async_computation.3 | async-start | bytes 294912 | tf_op jit(solution)/shard_map/reduce_scatter | solution.py:133
  110.1 493.7 %all-reduce.4.cloned.1.call-start = ((), (), s32[]{:S(2)}) async-start(), calls=%async_computation.2 | async-start | bytes 4194304 | tf_op jit(solution)/shard_map/psum | solution.py:135
Sparse Core Ops, SparseCore 0:
  108.4 227.2 all-reduce.5
  341.6 262.1 all-reduce.3
Sparse Core Ops, SparseCore 1:
  111.2 77.4 reduce-scatter.6
  191.1 35.7 reduce-scatter.4
where the time goes:
time: 616 us; the launch traced here: 614 us
  waiting for transfers between devices  352 us (57%)
  blocking collectives  205 us (33%)
  local copies, waits for them, and re-layouts  19.5 us (3%)
  between operations  16.2 us (3%)
  matrix products  11.8 us (2%)
    unnamed x6, waiting for transfers between devices  224 us
    psum x1, waiting for transfers between devices, on_device(): core_gradient = lax.psum(core_sum, ('ia', 'ja', 'ka'))  127 us
    psum x1, blocking collectives, on_device(): depth_whole = lax.psum(depth_sum, ('ia', 'ja'))  125 us
    all_gather x1, blocking collectives, on_device(): row_table = lax.all_gather(factor_rows, ('ja', 'ka'), axis=1, tiled=True)  48 us
    all_gather x1, blocking collectives, on_device(): col_table = lax.all_gather(factor_cols, 'ka', axis=1, tiled=True)  18.2 us
    psum x1, blocking collectives, on_device(): cols_whole = lax.psum(cols_sum, 'ia')  13.9 us
  transfers between devices with their start and end apart: 4, of which 2 were waited for; matrix products, arithmetic and copies ran while one was open for 1% of the time, Pallas kernels for 0%

commit v1 on v0

v1 whole, which is shorter than its diff:
```python
import jax
import jax.numpy as jnp
from jax import lax
from jax.experimental import pallas as pl
from jax.experimental.pallas import tpu as pltpu
from jax.sharding import PartitionSpec as P

MESH = pl.DeviceIdType.MESH
f32 = jnp.float32
bf16 = jnp.bfloat16
resid_scale = 1.0 / 64.0

NN = (((1,), (0,)), ((), ()))
NT = (((1,), (1,)), ((), ()))
TN = (((0,), (0,)), ((), ()))


def dot(a, b, dims=NN):
    return lax.dot_general(a, b, dims, preferred_element_type=f32)


def lane_low(shape):
    return lax.broadcasted_iota(jnp.int32, shape, len(shape) - 1) < 64


def two_terms(value):
    lead = value.astype(bf16).astype(f32)
    return jnp.where(lane_low(value.shape), lead, value - lead).astype(bf16)


def unit(size):
    return (
        lax.broadcasted_iota(jnp.int32, (size, size), 0)
        == lax.broadcasted_iota(jnp.int32, (size, size), 1)
    ).astype(bf16)


def gather_kernel(
    rows_ref, cols_ref, depth_ref, core_ref,
    row_out, col_out, slab_out, first_out,
    row_buf, col_buf, first_buf, send_sem, recv_sem,
):
    ja = lax.axis_index("ja")
    ka = lax.axis_index("ka")
    own_rows = rows_ref[...]
    own_cols = cols_ref[...]
    row_buf[ja, pl.ds(pl.multiple_of(ka * 16, 16), 16), :] = dot(
        unit(16), jnp.concatenate([own_rows, own_rows], axis=0), NT
    ).astype(bf16)
    col_buf[ka] = dot(unit(64), jnp.concatenate([own_cols, own_cols], axis=0), NT).astype(bf16)

    barrier = pltpu.get_barrier_semaphore()
    for step in range(1, 8):
        pl.semaphore_signal(barrier, inc=1, device_id={"ka": (ka + step) % 8}, device_id_type=MESH)
        pl.semaphore_signal(barrier, inc=1, device_id={"ja": (ja + step) % 8}, device_id_type=MESH)
    pl.semaphore_wait(barrier, 14)

    def send(ref, slot, target):
        copy = pltpu.make_async_remote_copy(
            src_ref=ref, dst_ref=ref, send_sem=send_sem.at[slot], recv_sem=recv_sem.at[slot],
            device_id=target, device_id_type=MESH,
        )
        copy.start()
        return copy

    own_tile = row_buf.at[ja, pl.ds(pl.multiple_of(ka * 16, 16), 16), :]
    deep_rows = [send(own_tile, step - 1, {"ka": (ka + step) % 8}) for step in range(1, 8)]
    deep_cols = [send(col_buf.at[ka], step + 6, {"ka": (ka + step) % 8}) for step in range(1, 8)]

    slab = depth_ref[:, pl.ds(pl.multiple_of(ka * 128, 128), 128)]
    slab_out[...] = slab
    slab_rows = dot(unit(128), slab, NT).astype(bf16)

    def first_of(r1, carry):
        piece = core_ref[r1]
        first_buf[pl.ds(r1, 128, stride=64), :] = dot(
            slab_rows, jnp.concatenate([piece, piece], axis=0), NT
        )
        return carry

    lax.fori_loop(0, 64, first_of, 0, unroll=8)

    for copy in deep_rows:
        copy.wait_recv()
    wide_rows = [send(row_buf.at[ja], step + 13, {"ja": (ja + step) % 8}) for step in range(1, 8)]

    def round_of(step, carry):
        part = pl.ds(pl.multiple_of(step * 256, 256), 256)
        first_out[part, :] = first_buf[part, :].astype(bf16)
        return carry

    lax.fori_loop(0, 32, round_of, 0, unroll=2)

    for copy in deep_cols:
        copy.wait_recv()
    col_out[...] = col_buf[...]
    for copy in wide_rows:
        copy.wait_recv()
    row_out[...] = row_buf[...]
    for copy in deep_rows + deep_cols + wide_rows:
        copy.wait_send()


def gather_factors(factor_rows, factor_cols, factor_depth, core_tensor):
    vmem = pl.BlockSpec(memory_space=pltpu.VMEM)
    return pl.pallas_call(
        gather_kernel,
        out_shape=(
            jax.ShapeDtypeStruct((8, 128, 128), bf16),
            jax.ShapeDtypeStruct((8, 64, 128), bf16),
            jax.ShapeDtypeStruct((64, 128), bf16),
            jax.ShapeDtypeStruct((8192, 128), bf16),
        ),
        in_specs=[vmem] * 4,
        out_specs=(vmem,) * 4,
        scratch_shapes=[
            pltpu.VMEM((8, 128, 128), bf16),
            pltpu.VMEM((8, 64, 128), bf16),
            pltpu.VMEM((8192, 128), f32),
            pltpu.SemaphoreType.DMA((21,)),
            pltpu.SemaphoreType.DMA((21,)),
        ],
        compiler_params=pltpu.CompilerParams(
            collective_id=0, has_side_effects=True, vmem_limit_bytes=32 << 20
        ),
        name="gather_factors",
    )(factor_rows, factor_cols, factor_depth, core_tensor)


def block_kernel(
    coords, counts,
    data_ref, weight_ref, first_ref, row_ref, col_ref, slab_ref, core_ref,
    core_out, rows_out, cols_out, depth_out,
    mid, back_sum, col_sum,
):
    slot = pl.program_id(0)

    @pl.when(slot == 0)
    def _():
        rows_out[...] = jnp.zeros_like(rows_out)
        back_sum[...] = jnp.zeros_like(back_sum)
        col_sum[...] = jnp.zeros_like(col_sum)

    @pl.when(slot < counts[0])
    def _():
        p = coords[slot * 3] & 7
        q = coords[slot * 3 + 1] & 3
        t = coords[slot * 3 + 2] & 3
        row_t = row_ref[p][:, :64]
        col_t = col_ref[pl.ds(q * 2, 2)].reshape(128, 128)
        row_n = dot(unit(64), row_t, NT).astype(bf16)
        first_base = t * 2048

        def first_pair(pair):
            k = pair * 2
            at = pl.multiple_of(first_base + k * 64, 128)
            both = first_ref[pl.ds(at, 128), :]
            return k, jnp.concatenate([both[:64], both[64:]], axis=1)

        def forward(pair, carry):
            k, pair_first = first_pair(pair)
            part = dot(row_t, pair_first)
            mid[pl.ds(k, 128, stride=32), :] = part[:, :128]
            mid[pl.ds(k + 1, 128, stride=32), :] = part[:, 128:]
            return carry

        lax.fori_loop(0, 16, forward, 0, unroll=4)

        def middle(step, col_part):
            part = pl.ds(pl.multiple_of(step * 256, 256), 256)
            lead_rest = two_terms(mid[part, :])
            model = dot(lead_rest, col_t, NT)
            residual = (
                weight_ref[0, part, :].astype(f32)
                * (model - data_ref[0, part, :].astype(f32))
                * resid_scale
            ).astype(bf16)
            mid[part, :] = dot(residual, col_t)
            return col_part + dot(lead_rest, residual, TN)

        col_part = lax.fori_loop(0, 16, middle, jnp.zeros((128, 128), f32), unroll=4)
        col_sum[q] += col_part[:64] + col_part[64:]

        def backward(pair, row_part):
            k, pair_first = first_pair(pair)
            back = jnp.concatenate(
                [
                    two_terms(mid[pl.ds(k, 128, stride=32), :]),
                    two_terms(mid[pl.ds(k + 1, 128, stride=32), :]),
                ],
                axis=1,
            )
            both = dot(row_n, back)
            for half in range(2):
                piece = both[:, half * 128 : half * 128 + 128]
                piece = piece + pltpu.roll(piece, 64, axis=1)
                piece = jnp.where(lane_low((32, 128)), piece[:32], piece[32:])
                at = pl.multiple_of((t * 32 + k + half) * 32, 32)
                back_sum[pl.ds(at, 32), :] += piece.astype(bf16).astype(f32)
            return row_part + dot(pair_first, back, NT)

        row_part = lax.fori_loop(0, 16, backward, jnp.zeros((64, 128), f32), unroll=4)
        rows_out[p] += row_part

    @pl.when(slot == pl.num_programs(0) - 1)
    def _():
        cols_out[...] = col_sum[...]
        slab = slab_ref[...]
        slab_twice = jnp.concatenate([slab, slab], axis=1)

        def finish(u, depth_part):
            value = back_sum[pl.ds(u, 128, stride=32), :]
            lead = value.astype(bf16)
            rest = (value - lead.astype(f32)).astype(bf16)
            core_out[u] = dot(slab_twice, jnp.concatenate([lead, rest], axis=0))
            piece = jnp.concatenate([core_ref[u], core_ref[u + 32]], axis=0)
            return depth_part + dot(lead, piece) + dot(rest, piece)

        depth_part = lax.fori_loop(0, 32, finish, jnp.zeros((128, 64), f32), unroll=4)
        depth_out[...] = jnp.concatenate(
            [depth_part, jnp.zeros((128, 64), f32)], axis=1
        ).T[:64]


def block_gradients(coords, counts, data, weights, first, rows, cols, slab, core_tensor):
    slots = data.shape[0]

    def live(slot, coords, counts):
        return (jnp.minimum(slot, jnp.maximum(counts[0] - 1, 0)), 0, 0)

    def whole(shape):
        zeros = (0,) * len(shape)
        return pl.BlockSpec(shape, lambda slot, coords, counts: zeros)

    return pl.pallas_call(
        block_kernel,
        out_shape=(
            jax.ShapeDtypeStruct((32, 64, 128), f32),
            jax.ShapeDtypeStruct((8, 64, 128), f32),
            jax.ShapeDtypeStruct((4, 64, 128), f32),
            jax.ShapeDtypeStruct((64, 128), f32),
        ),
        grid_spec=pltpu.PrefetchScalarGridSpec(
            num_scalar_prefetch=2,
            grid=(slots,),
            in_specs=[
                pl.BlockSpec((1, 4096, 128), live),
                pl.BlockSpec((1, 4096, 128), live),
                whole((8192, 128)),
                whole((8, 128, 128)),
                whole((8, 64, 128)),
                whole((64, 128)),
                whole((64, 64, 64)),
            ],
            out_specs=(
                whole((32, 64, 128)),
                whole((8, 64, 128)),
                whole((4, 64, 128)),
                whole((64, 128)),
            ),
            scratch_shapes=[
                pltpu.VMEM((4096, 128), f32),
                pltpu.VMEM((4096, 128), f32),
                pltpu.VMEM((4, 64, 128), f32),
            ],
        ),
        compiler_params=pltpu.CompilerParams(
            dimension_semantics=("arbitrary",), vmem_limit_bytes=48 << 20
        ),
        name="block_gradients",
    )(coords, counts, data, weights, first, rows, cols, slab, core_tensor)


def reduce_kernel(
    core_ref, rows_ref, cols_ref, depth_ref,
    core_out, rows_out, cols_out, depth_out,
    core_pair, core_sum, core_x, core_y, half_x, half_y, end_y, end_x, tile_sum, tile_in, tile_all, core_all,
    rows_pair, rows_sum, rows_x, rows_t, rows_z,
    cols_y, cols_sum, cols_z, cols_all,
    depth_pair, depth_sum, depth_x, depth_one, depth_y, depth_all,
    send_sem, recv_sem,
):
    y = lax.axis_index("ia")
    ja = lax.axis_index("ja")
    z = lax.axis_index("ka")
    x = ja // 2
    c = ja % 2
    o = 1 - c
    low = pl.ds(0, 32)
    high = pl.ds(32, 32)

    barrier = pltpu.get_barrier_semaphore()

    def mate():
        return {"ja": x * 2 + o}

    def on_x(step):
        return {"ja": ((x + step) % 4) * 2 + c}

    def on_y(step):
        return {"ia": (y + step) % 4}

    def on_z(step):
        return {"ka": (z + step) % 8}

    targets = [mate()] + [on_x(s) for s in (1, 2, 3)] + [on_y(s) for s in (1, 2, 3)]
    targets += [on_z(s) for s in range(1, 8)]
    for target in targets:
        pl.semaphore_signal(barrier, inc=1, device_id=target, device_id_type=MESH)
    pl.semaphore_wait(barrier, len(targets))

    started = []

    def send(src, dst, target):
        slot = len(started)
        copy = pltpu.make_async_remote_copy(
            src_ref=src, dst_ref=dst, send_sem=send_sem.at[slot], recv_sem=recv_sem.at[slot],
            device_id=target, device_id_type=MESH,
        )
        copy.start()
        started.append(copy)
        return copy

    def arrived(copies):
        for copy in copies:
            copy.wait_recv()

    core_c0 = send(core_ref.at[o, :, :, low], core_pair.at[:, :, low], mate())
    core_c1 = send(core_ref.at[o, :, :, high], core_pair.at[:, :, high], mate())
    rows_c = send(rows_ref.at[:, o], rows_pair, mate())
    depth_c = send(depth_ref.at[o], depth_pair, mate())
    cols_s1 = [
        send(cols_ref.at[:, pl.ds(pl.multiple_of(((y + s) % 4) * 16, 16), 16), :], cols_y.at[s - 1], on_y(s))
        for s in (1, 2, 3)
    ]

    core_c0.wait_recv()
    core_sum[:, :, low] = core_ref[c, :, :, low] + core_pair[:, :, low]
    core_x0 = [send(core_sum.at[(x + s) % 4, :, low], core_x.at[s - 1], on_x(s)) for s in (1, 2, 3)]
    core_c1.wait_recv()
    core_sum[:, :, high] = core_ref[c, :, :, high] + core_pair[:, :, high]
    core_y1 = [send(core_sum.at[:, (y + s) % 4, high], core_y.at[s - 1], on_y(s)) for s in (1, 2, 3)]
    rows_c.wait_recv()
    rows_sum[...] = rows_ref[:, c] + rows_pair[...]
    rows_s1 = [send(rows_sum.at[(x + s) % 4], rows_x.at[s - 1], on_x(s)) for s in (1, 2, 3)]
    depth_c.wait_recv()
    depth_sum[...] = depth_ref[c] + depth_pair[...]
    depth_s1 = [send(depth_sum.at[(x + s) % 4], depth_x.at[s - 1], on_x(s)) for s in (1, 2, 3)]

    arrived(cols_s1)
    cols_sum[...] = (
        cols_ref[:, pl.ds(pl.multiple_of(y * 16, 16), 16), :] + cols_y[0] + cols_y[1] + cols_y[2]
    )
    cols_s2 = [send(cols_sum.at[((z + s) % 8) // 2], cols_z.at[s - 1], on_z(s)) for s in range(1, 8)]

    arrived(core_x0)
    half_x[...] = core_sum[x, :, low] + core_x[0] + core_x[1] + core_x[2]
    core_y0 = [send(half_x.at[(y + s) % 4], end_y.at[s - 1], on_y(s)) for s in (1, 2, 3)]
    arrived(core_y1)
    half_y[...] = core_sum[:, y, high] + core_y[0] + core_y[1] + core_y[2]
    core_x1 = [send(half_y.at[(x + s) % 4], end_x.at[s - 1], on_x(s)) for s in (1, 2, 3)]

    arrived(rows_s1)
    rows_own = rows_sum[x] + rows_x[0] + rows_x[1] + rows_x[2]
    rows_t[...] = jnp.concatenate([rows_own, jnp.zeros((64, 128), f32)], axis=0).T
    rows_s2 = [
        send(rows_t.at[pl.ds(pl.multiple_of(((z + s) % 8) * 16, 16), 16), :], rows_z.at[s - 1], on_z(s))
        for s in range(1, 8)
    ]
    arrived(depth_s1)
    depth_one[...] = depth_sum[x] + depth_x[0] + depth_x[1] + depth_x[2]
    depth_s2 = [send(depth_one, depth_y.at[s - 1], on_y(s)) for s in (1, 2, 3)]

    arrived(core_y0)
    tile_sum[low] = half_x[y] + end_y[0] + end_y[1] + end_y[2]
    arrived(core_x1)
    tile_sum[high] = half_y[x] + end_x[0] + end_x[1] + end_x[2]
    core_z = [
        send(tile_sum.at[pl.ds(pl.multiple_of(((z + s) % 8) * 8, 8), 8), :], tile_in.at[s - 1], on_z(s))
        for s in range(1, 8)
    ]

    arrived(cols_s2)
    col_total = cols_sum[z // 2]
    for s in range(7):
        col_total = col_total + cols_z[s]
    cols_all[y] = col_total
    cols_s3 = [send(cols_all.at[y], cols_all.at[y], on_y(s)) for s in (1, 2, 3)]
    arrived(depth_s2)
    depth_all[c, x] = depth_one[...] + depth_y[0] + depth_y[1] + depth_y[2]
    depth_s3 = [send(depth_all.at[c, x], depth_all.at[c, x], on_x(s)) for s in (1, 2, 3)]
    arrived(rows_s2)
    row_total = rows_t[pl.ds(pl.multiple_of(z * 16, 16), 16), :]
    for s in range(7):
        row_total = row_total + rows_z[s]
    rows_out[...] = jnp.concatenate([row_total, jnp.zeros((112, 128), f32)], axis=0).T[:64, :16]

    own = pl.ds(pl.multiple_of(z * 8, 8), 8)
    arrived(core_z)
    total = tile_sum[own, :]
    for s in range(7):
        total = total + tile_in[s]
    tile_all[own, :] = total
    core_g = [send(tile_all.at[own, :], tile_all.at[own, :], on_z(s)) for s in range(1, 8)]
    arrived(depth_s3)
    depth_s4 = send(depth_all.at[c], depth_all.at[c], mate())
    arrived(core_g)
    turned = jnp.concatenate([tile_all[...], jnp.zeros((64, 128), f32)], axis=0).T
    core_all[c, x, y] = turned[:64] + pltpu.roll(turned[64:], 64, axis=1)

    back_y0 = [send(core_all.at[c, x, y, low], core_all.at[c, x, y, low], on_y(s)) for s in (1, 2, 3)]
    back_x1 = [send(core_all.at[c, x, y, high], core_all.at[c, x, y, high], on_x(s)) for s in (1, 2, 3)]
    arrived(back_y0)
    back_x0 = [send(core_all.at[c, x, :, low], core_all.at[c, x, :, low], on_x(s)) for s in (1, 2, 3)]
    arrived(back_x1)
    back_y1 = [send(core_all.at[c, :, y, high], core_all.at[c, :, y, high], on_y(s)) for s in (1, 2, 3)]

    arrived(cols_s3)
    whole = cols_all[...].reshape(64, 128)
    cols_out[...] = jnp.where(z % 2 == 1, pltpu.roll(whole, 64, axis=1), whole)[:, :64]

    arrived(back_x0)
    back_c0 = send(core_all.at[c, :, :, low], core_all.at[c, :, :, low], mate())
    arrived(back_y1)
    back_c1 = send(core_all.at[c, :, :, high], core_all.at[c, :, :, high], mate())
    depth_s4.wait_recv()
    depth_out[...] = depth_all[...].reshape(64, 128)
    core_out[c] = core_all[c]
    back_c0.wait_recv()
    back_c1.wait_recv()
    core_out[o] = core_all[o]
    for copy in started:
        copy.wait_send()


def reduce_gradients(core, rows, cols, depth):
    vmem = pl.BlockSpec(memory_space=pltpu.VMEM)
    copies = 95

    def buf(*shape):
        return pltpu.VMEM(shape, f32)

    return pl.pallas_call(
        reduce_kernel,
        out_shape=(
            jax.ShapeDtypeStruct((2, 4, 4, 64, 128), f32),
            jax.ShapeDtypeStruct((64, 16), f32),
            jax.ShapeDtypeStruct((64, 64), f32),
            jax.ShapeDtypeStruct((64, 128), f32),
        ),
        in_specs=[vmem] * 4,
        out_specs=(vmem,) * 4,
        scratch_shapes=[
            buf(4, 4, 64, 128),
            buf(4, 4, 64, 128),
            buf(3, 4, 32, 128),
            buf(3, 4, 32, 128),
            buf(4, 32, 128),
            buf(4, 32, 128),
            buf(3, 32, 128),
            buf(3, 32, 128),
            buf(64, 128),
            buf(7, 8, 128),
            buf(64, 128),
            buf(2, 4, 4, 64, 128),
            buf(4, 64, 128),
            buf(4, 64, 128),
            buf(3, 64, 128),
            buf(128, 128),
            buf(7, 16, 128),
            buf(3, 4, 16, 128),
            buf(4, 16, 128),
            buf(7, 16, 128),
            buf(4, 16, 128),
            buf(4, 8, 128),
            buf(4, 8, 128),
            buf(3, 8, 128),
            buf(8, 128),
            buf(3, 8, 128),
            buf(2, 4, 8, 128),
            pltpu.SemaphoreType.DMA((copies,)),
            pltpu.SemaphoreType.DMA((copies,)),
        ],
        compiler_params=pltpu.CompilerParams(
            collective_id=1, has_side_effects=True, vmem_limit_bytes=32 << 20
        ),
        name="reduce_gradients",
    )(core, rows, cols, depth)


def on_device(
    observed, weights, coords, counts, factor_rows, factor_cols, factor_depth, core_tensor
):
    slots = observed.shape[2]
    data = observed.reshape(slots, 4096, 128)
    weight = weights.reshape(slots, 4096, 128)
    rows, cols, slab, first = gather_factors(factor_rows, factor_cols, factor_depth, core_tensor)
    core_part, rows_part, cols_part, depth_part = block_gradients(
        coords.reshape(slots * 3), counts.reshape(1), data, weight, first, rows, cols, slab, core_tensor
    )
    core, rows_gradient, cols_gradient, depth_gradient = reduce_gradients(
        core_part.reshape(2, 4, 4, 64, 128),
        rows_part.reshape(4, 2, 64, 128),
        cols_part,
        depth_part.reshape(2, 4, 8, 128),
    )
    core = core.reshape(32, 64, 128)
    core_gradient = jnp.concatenate([core[:, :, :64], core[:, :, 64:]], axis=0)
    return (rows_gradient, cols_gradient, depth_gradient, core_gradient)


def solution(mesh):
    in_specs = (
        P("ia", "ja", "ka", None, None, None),
        P("ia", "ja", "ka", None, None, None),
        P("ia", "ja", "ka", None),
        P("ia", "ja", "ka"),
        P(None, ("ia", "ja", "ka")),
        P(None, ("ja", "ka")),
        P(),
        P(),
    )
    out_specs = (P(None, ("ia", "ja", "ka")), P(None, ("ja", "ka")), P(None, "ka"), P())
    return jax.shard_map(
        on_device, mesh=mesh, in_specs=in_specs, out_specs=out_specs, check_vma=False
    )
```

time: 616 us -> 106 us (0.17)
  waiting for transfers between devices: 352 us -> 0 us
  blocking collectives: 205 us -> 0 us
  Pallas kernels: 0 us -> 94.7 us
  between operations: 16.2 us -> 1.33 us
  matrix products: 11.8 us -> 0 us
  local copies, waits for them, and re-layouts: 19.5 us -> 7.96 us
    unnamed x6 -> x0, waiting for transfers between devices: 224 us -> none
    psum x2 -> x0, blocking collectives: 139 us -> none  [the longest x1 125 us: on_device(): depth_whole = lax.psum(depth_sum, ('ia', 'ja'))]
    psum x1 -> x0, waiting for transfers between devices: 127 us -> none  [on_device(): core_gradient = lax.psum(core_sum, ('ia', 'ja', 'ka'))]
    pallas_call x0 -> x3, Pallas kernels: none -> 94.7 us  [the longest x1 55.9 us: reduce_gradients(): pl.pallas_call(reduce_kernel, out_shape=(jax.ShapeDtypeStruct((2, 4, 4, 6...]
    all_gather x2 -> x0, blocking collectives: 66.2 us -> none  [the longest x1 48 us: on_device(): row_table = lax.all_gather(factor_rows, ('ja', 'ka'), axis=1, tiled=True)]
    dot_general x18 -> x0, matrix products: 11.8 us -> none  [the longest x2 5.34 us: block_terms(): lax.dot_general(row_factor, second_flat, (((0,), (0,)), ((), ())), prefer...]
    while x15 -> x0, local copies, waits for them, and re-layouts: 7.22 us -> none
  transfers between devices with their start and end apart: 4 -> 0, of which waited for: 2 -> 0; matrix products, arithmetic and copies ran while one was open for 1% -> 0% of each run, Pallas kernels for 0% -> 0%
where the time goes in v1:
time: 106 us; the launch traced here: 105 us
  Pallas kernels  94.7 us (89%)
  local copies, waits for them, and re-layouts  7.96 us (8%)
  other arithmetic  1.49 us (1%)
  between operations  1.33 us (1%)
    pallas_call x1, Pallas kernels, reduce_gradients(): pl.pallas_call(reduce_kernel, out_shape=(jax.ShapeDtypeStruct((2, 4, 4, 6...  55.9 us
    pallas_call x1, Pallas kernels, gather_factors(): pl.pallas_call(gather_kernel, out_shape=(jax.ShapeDtypeStruct((8, 128, 12...  19.5 us
    pallas_call x1, Pallas kernels, block_gradients(): pl.pallas_call(block_kernel, out_shape=(jax.ShapeDtypeStruct((32, 64, 128...  19.3 us
    unnamed x13, local copies, waits for them, and re-layouts  7.51 us

profile of v1, /device:TPU:1, one launch (start us, length us, event | category | flops | bytes accessed | tf_op | source)
XLA Modules:
  0.0 105.5 jit_solution(2481171484438006257)
XLA Ops:
  1.3 0.8 copy.15
  2.0 0.1 reshape.32.coords
  2.1 0.8 copy.16.rows_ref
  2.9 0.0 copy-start
  2.9 1.2 %copy-done = bf16[64,64,64]{2,1,0:T(8,128)(2,1)S(1)} copy-done((bf16[64,64,64]{2,1,0:T(8,128)(2,1)S(1)}, bf16[64,64,64]{2,1,0:T(8,128)(2,1)}, u32[]{:S(2)}) %copy-start) | copy-done | bytes 524312
  4.1 0.0 copy-start.2
  4.1 0.9 copy-done.2
  5.0 0.0 copy-start.3
  5.0 0.7 copy-done.3
  5.8 19.5 %gather_factors.1 = (bf16[8,128,128]{2,1,0:T(8,128)(2,1)S(1)}, bf16[8,64,128]{2,1,0:T(8,128)(2,1)S(1)}, bf16[64,128]{1,0:T(8,128)(2,1)S(1)}, bf16[8192,128]{1,0:T(8,128)(2,1)S(1)}) custom-call(bf16[64,16]{1,0:T(8,128)(2,1)S(1)} %copy.16.rows_ref, bf16[64,64]{1,0:T(8,128)(2,1)S(1)} %copy-done.3, bf16[64,1024]{1,0:T(8,128)(2,1)S(1)} %copy-done.2, ...), custom_call_target="tpu_custom_call" | custom-call | tf_op jit(solution)/shard_map/gather_factors/pallas_call | solution.py:106
  25.3 0.0 copy-start.1
  25.3 1.2 %copy-done.1 = bf16[64,64,64]{2,1,0:T(8,128)(2,1)S(1)} copy-done((bf16[64,64,64]{2,1,0:T(8,128)(2,1)S(1)}, bf16[64,64,64]{2,1,0:T(8,128)(2,1)}, u32[]{:S(2)}) %copy-start.1) | copy-done | bytes 524312
  26.5 19.3 %block_gradients.1 = (f32[32,64,128]{2,1,0:T(8,128)S(1)}, f32[8,64,128]{2,1,0:T(8,128)S(1)}, f32[4,64,128]{2,1,0:T(8,128)S(1)}, f32[64,128]{1,0:T(8,128)S(1)}) custom-call(s32[15]{0:T(128)S(1)} %reshape.32.coords, s32[1]{0:T(128)} %bitcast.7.counts, bf16[5,4096,128]{2,1,0:T(8,128)(2,1)} %bitcast.12, bf16[5,4096,128]{2,1,0:T(8,128)(2,1)} %bitcast.13, ...), custom_call_target="tpu_custom_call" | custom-call | tf_op jit(solution)/shard_map/block_gradients/pallas_call | solution.py:235
  45.8 55.9 %reduce_gradients.1 = (f32[2,4,4,64,128]{4,3,2,1,0:T(8,128)S(1)}, f32[64,16]{1,0:T(8,128)S(1)}, f32[64,64]{1,0:T(8,128)S(1)}, f32[64,128]{1,0:T(8,128)S(1)}) custom-call(f32[2,4,4,64,128]{4,3,2,1,0:T(8,128)S(1)} %bitcast.9, f32[4,2,64,128]{3,2,1,0:T(8,128)S(1)} %bitcast.10, f32[4,64,128]{2,1,0:T(8,128)S(1)} %get-tuple-element.22.cols_ref, ...), custom_call_target="tpu_custom_call" | custom-call | tf_op jit(solution)/shard_map/reduce_gradients/pallas_call | solution.py:443
  101.7 0.7 copy.17
  102.4 0.4 fusion
  102.8 1.5 %pad_maximum_fusion = f32[64,64,64]{2,1,0:T(8,128)} fusion(f32[32,64,64]{2,1,0:T(8,128)S(1)} %get-tuple-element.37, f32[32,64,64]{2,1,0:T(8,128)S(1)} %get-tuple-element.36), kind=kLoop, calls=%fused_computation | loop fusion | flops 262144 | bytes 2097152 | tf_op jit(solution)/shard_map/concatenate | solution.py:508
  104.3 0.6 copy.21
  104.9 0.6 copy.22
Async XLA Ops:
  2.9 1.2 %copy-start = (bf16[64,64,64]{2,1,0:T(8,128)(2,1)S(1)}, bf16[64,64,64]{2,1,0:T(8,128)(2,1)}, u32[]{:S(2)}) copy-start(bf16[64,64,64]{2,1,0:T(8,128)(2,1)} %core_ref.3) | copy-start | bytes 1572868
  4.1 0.9 copy-start.2
  5.0 0.7 copy-start.3
  25.3 1.2 %copy-start.1 = (bf16[64,64,64]{2,1,0:T(8,128)(2,1)S(1)}, bf16[64,64,64]{2,1,0:T(8,128)(2,1)}, u32[]{:S(2)}) copy-start(bf16[64,64,64]{2,1,0:T(8,128)(2,1)} %core_ref.3) | copy-start | bytes 1572868

commit v2 on v1

--- a/solution.py
+++ b/solution.py
@@ -19,13 +19,8 @@
     return lax.dot_general(a, b, dims, preferred_element_type=f32)
 
 
-def lane_low(shape):
+def low_lanes(shape):
     return lax.broadcasted_iota(jnp.int32, shape, len(shape) - 1) < 64
-
-
-def two_terms(value):
-    lead = value.astype(bf16).astype(f32)
-    return jnp.where(lane_low(value.shape), lead, value - lead).astype(bf16)
 
 
 def unit(size):
@@ -35,24 +30,50 @@
     ).astype(bf16)
 
 
+def twice(value, axis):
+    return jnp.concatenate([value, value], axis=axis)
+
+
+def split_terms(value):
+    lead = value.astype(bf16)
+    return lead, (value - lead.astype(f32)).astype(bf16)
+
+
+def half_first(value):
+    return jnp.concatenate(
+        [value[t * 32 + half * 16 : t * 32 + half * 16 + 16] for half in range(2) for t in range(4)], axis=0
+    )
+
+
+def half_inside(value):
+    return jnp.concatenate(
+        [value[half * 64 + t * 16 : half * 64 + t * 16 + 16] for t in range(4) for half in range(2)], axis=0
+    )
+
+
 def gather_kernel(
-    rows_ref, cols_ref, depth_ref, core_ref,
+    rows_ref, cols_ref, depth_hbm, core_hbm,
     row_out, col_out, slab_out, first_out,
-    row_buf, col_buf, first_buf, send_sem, recv_sem,
+    row_buf, col_buf, first_buf, slab_in, core_in, send_sem, recv_sem, local_sem,
 ):
     ja = lax.axis_index("ja")
     ka = lax.axis_index("ka")
-    own_rows = rows_ref[...]
-    own_cols = cols_ref[...]
-    row_buf[ja, pl.ds(pl.multiple_of(ka * 16, 16), 16), :] = dot(
-        unit(16), jnp.concatenate([own_rows, own_rows], axis=0), NT
-    ).astype(bf16)
-    col_buf[ka] = dot(unit(64), jnp.concatenate([own_cols, own_cols], axis=0), NT).astype(bf16)
+    core_copy = pltpu.make_async_copy(core_hbm, core_in, local_sem.at[0])
+    core_copy.start()
+    slab_copy = pltpu.make_async_copy(
+        depth_hbm.at[:, pl.ds(pl.multiple_of(ka * 128, 128), 128)], slab_in, local_sem.at[1]
+    )
+    slab_copy.start()
 
     barrier = pltpu.get_barrier_semaphore()
     for step in range(1, 8):
         pl.semaphore_signal(barrier, inc=1, device_id={"ka": (ka + step) % 8}, device_id_type=MESH)
         pl.semaphore_signal(barrier, inc=1, device_id={"ja": (ja + step) % 8}, device_id_type=MESH)
+
+    own_rows = dot(rows_ref[...], twice(unit(64), 1))
+    row_buf[ja, ka] = jnp.where(low_lanes((8, 128)), own_rows[:8], own_rows[8:]).astype(bf16)
+    own_cols = dot(unit(64), twice(cols_ref[...], 0), NT)
+    col_buf[ka] = jnp.where(low_lanes((32, 128)), own_cols[:32], own_cols[32:]).astype(bf16)
     pl.semaphore_wait(barrier, 14)
 
     def send(ref, slot, target):
@@ -63,33 +84,37 @@
         copy.start()
         return copy
 
-    own_tile = row_buf.at[ja, pl.ds(pl.multiple_of(ka * 16, 16), 16), :]
-    deep_rows = [send(own_tile, step - 1, {"ka": (ka + step) % 8}) for step in range(1, 8)]
-    deep_cols = [send(col_buf.at[ka], step + 6, {"ka": (ka + step) % 8}) for step in range(1, 8)]
-
-    slab = depth_ref[:, pl.ds(pl.multiple_of(ka * 128, 128), 128)]
-    slab_out[...] = slab
-    slab_rows = dot(unit(128), slab, NT).astype(bf16)
-
-    def first_of(r1, carry):
-        piece = core_ref[r1]
-        first_buf[pl.ds(r1, 128, stride=64), :] = dot(
-            slab_rows, jnp.concatenate([piece, piece], axis=0), NT
-        )
+    order = (4, 3, 5, 2, 6, 1, 7)
+    deep_rows = [send(row_buf.at[ja, ka], step - 1, {"ka": (ka + step) % 8}) for step in order]
+    deep_cols = [send(col_buf.at[ka], step + 6, {"ka": (ka + step) % 8}) for step in order]
+
+    slab_copy.wait()
+    slab_rows = half_first(dot(unit(128), slab_in[...], NT).astype(bf16))
+    slab_out[...] = dot(unit(64), slab_rows, NT).astype(bf16)
+    core_copy.wait()
+
+    def first_of(pair, carry):
+        left = core_in[pair * 2]
+        right = core_in[pair * 2 + 1]
+        both = dot(slab_rows, jnp.concatenate([left, left, right, right], axis=0), NT)
+        for side in range(2):
+            piece = both[:, side * 128 : side * 128 + 128]
+            first_buf[pl.ds(pair * 2 + side, 64, stride=65), :] = jnp.where(
+                low_lanes((64, 128)), piece[:64], piece[64:]
+            )
         return carry
 
-    lax.fori_loop(0, 64, first_of, 0, unroll=8)
+    lax.fori_loop(0, 32, first_of, 0, unroll=4)
 
     for copy in deep_rows:
         copy.wait_recv()
-    wide_rows = [send(row_buf.at[ja], step + 13, {"ja": (ja + step) % 8}) for step in range(1, 8)]
+    wide_rows = [send(row_buf.at[ja], step + 13, {"ja": (ja + step) % 8}) for step in order]
 
     def round_of(step, carry):
-        part = pl.ds(pl.multiple_of(step * 256, 256), 256)
-        first_out[part, :] = first_buf[part, :].astype(bf16)
+        first_out[step] = first_buf[pl.ds(step * 65, 64), :].astype(bf16)
         return carry
 
-    lax.fori_loop(0, 32, round_of, 0, unroll=2)
+    lax.fori_loop(0, 64, round_of, 0, unroll=8)
 
     for copy in deep_cols:
         copy.wait_recv()
@@ -103,25 +128,29 @@
 
 def gather_factors(factor_rows, factor_cols, factor_depth, core_tensor):
     vmem = pl.BlockSpec(memory_space=pltpu.VMEM)
+    hbm = pl.BlockSpec(memory_space=pltpu.HBM)
     return pl.pallas_call(
         gather_kernel,
         out_shape=(
-            jax.ShapeDtypeStruct((8, 128, 128), bf16),
-            jax.ShapeDtypeStruct((8, 64, 128), bf16),
+            jax.ShapeDtypeStruct((8, 8, 8, 128), bf16),
+            jax.ShapeDtypeStruct((8, 32, 128), bf16),
             jax.ShapeDtypeStruct((64, 128), bf16),
-            jax.ShapeDtypeStruct((8192, 128), bf16),
-        ),
-        in_specs=[vmem] * 4,
+            jax.ShapeDtypeStruct((64, 64, 128), bf16),
+        ),
+        in_specs=[vmem, vmem, hbm, hbm],
         out_specs=(vmem,) * 4,
         scratch_shapes=[
-            pltpu.VMEM((8, 128, 128), bf16),
-            pltpu.VMEM((8, 64, 128), bf16),
-            pltpu.VMEM((8192, 128), f32),
+            pltpu.VMEM((8, 8, 8, 128), bf16),
+            pltpu.VMEM((8, 32, 128), bf16),
+            pltpu.VMEM((64 * 65, 128), f32),
+            pltpu.VMEM((64, 128), bf16),
+            pltpu.VMEM((64, 64, 64), bf16),
             pltpu.SemaphoreType.DMA((21,)),
             pltpu.SemaphoreType.DMA((21,)),
+            pltpu.SemaphoreType.DMA((2,)),
         ],
         compiler_params=pltpu.CompilerParams(
-            collective_id=0, has_side_effects=True, vmem_limit_bytes=32 << 20
+            collective_id=0, has_side_effects=True, vmem_limit_bytes=33554432
         ),
         name="gather_factors",
     )(factor_rows, factor_cols, factor_depth, core_tensor)
@@ -129,104 +158,134 @@
 
 def block_kernel(
     coords, counts,
-    data_ref, weight_ref, first_ref, row_ref, col_ref, slab_ref, core_ref,
+    data_ref, weight_ref, first_ref, row_ref, col_ref, slab_ref, core_hbm,
     core_out, rows_out, cols_out, depth_out,
-    mid, back_sum, col_sum,
+    mid, back_sum, col_sum, core_in, core_sem,
 ):
     slot = pl.program_id(0)
+    last = pl.num_programs(0) - 1
+
+    def core_copy():
+        return pltpu.make_async_copy(core_hbm, core_in, core_sem)
 
     @pl.when(slot == 0)
     def _():
+        core_copy().start()
         rows_out[...] = jnp.zeros_like(rows_out)
         back_sum[...] = jnp.zeros_like(back_sum)
         col_sum[...] = jnp.zeros_like(col_sum)
 
-    @pl.when(slot < counts[0])
+    @pl.when(slot < counts[0, 0, 0])
     def _():
-        p = coords[slot * 3] & 7
-        q = coords[slot * 3 + 1] & 3
-        t = coords[slot * 3 + 2] & 3
-        row_t = row_ref[p][:, :64]
-        col_t = col_ref[pl.ds(q * 2, 2)].reshape(128, 128)
+        p = coords[0, 0, slot, 0] & 7
+        q = coords[0, 0, slot, 1] & 3
+        t = coords[0, 0, slot, 2] & 3
+        packed_rows = row_ref[p].astype(f32).reshape(64, 128)
+        turned_rows = pltpu.roll(packed_rows, 64, axis=1)
+        row_t = jnp.concatenate(
+            [part[z * 8 : z * 8 + 8] for z in range(8) for part in (packed_rows, turned_rows)], axis=0
+        )[:, :64].astype(bf16)
         row_n = dot(unit(64), row_t, NT).astype(bf16)
-        first_base = t * 2048
-
-        def first_pair(pair):
-            k = pair * 2
-            at = pl.multiple_of(first_base + k * 64, 128)
-            both = first_ref[pl.ds(at, 128), :]
-            return k, jnp.concatenate([both[:64], both[64:]], axis=1)
+        row_n2 = twice(row_n, 1)
+        packed_cols = col_ref[pl.ds(q * 2, 2)].astype(f32).reshape(64, 128)
+        turned_cols = pltpu.roll(packed_cols, 64, axis=1)
+        low = low_lanes((64, 128))
+        first_half = jnp.where(low, packed_cols, turned_cols)
+        second_half = jnp.where(low, turned_cols, packed_cols)
+        col_t = jnp.concatenate(
+            [first_half[:32], second_half[:32], first_half[32:], second_half[32:]], axis=0
+        )
+        low = low_lanes((128, 128))
+        zero = jnp.zeros((128, 128), f32)
+        col_low = jnp.where(low, col_t, zero)
+        col_high = jnp.where(low, zero, col_t)
+        to_model = jnp.concatenate([twice(col_low, 1), twice(col_high, 1)], axis=0).astype(bf16)
+        to_back = (jnp.concatenate([col_low, col_high], axis=0) * resid_scale).astype(bf16)
 
         def forward(pair, carry):
-            k, pair_first = first_pair(pair)
-            part = dot(row_t, pair_first)
-            mid[pl.ds(k, 128, stride=32), :] = part[:, :128]
-            mid[pl.ds(k + 1, 128, stride=32), :] = part[:, 128:]
+            kk = pair * 2
+            part = dot(
+                row_t, jnp.concatenate([first_ref[t * 16 + kk], first_ref[t * 16 + kk + 1]], axis=1)
+            )
+            mid[pl.ds(kk, 128, stride=17), :] = part[:, :128]
+            mid[pl.ds(kk + 1, 128, stride=17), :] = part[:, 128:]
             return carry
 
-        lax.fori_loop(0, 16, forward, 0, unroll=4)
+        lax.fori_loop(0, 8, forward, 0, unroll=FORWARD)
 
         def middle(step, col_part):
-            part = pl.ds(pl.multiple_of(step * 256, 256), 256)
-            lead_rest = two_terms(mid[part, :])
-            model = dot(lead_rest, col_t, NT)
-            residual = (
-                weight_ref[0, part, :].astype(f32)
-                * (model - data_ref[0, part, :].astype(f32))
-                * resid_scale
-            ).astype(bf16)
-            mid[part, :] = dot(residual, col_t)
-            return col_part + dot(lead_rest, residual, TN)
-
-        col_part = lax.fori_loop(0, 16, middle, jnp.zeros((128, 128), f32), unroll=4)
-        col_sum[q] += col_part[:64] + col_part[64:]
-
-        def backward(pair, row_part):
-            k, pair_first = first_pair(pair)
-            back = jnp.concatenate(
-                [
-                    two_terms(mid[pl.ds(k, 128, stride=32), :]),
-                    two_terms(mid[pl.ds(k + 1, 128, stride=32), :]),
-                ],
-                axis=1,
+            base = step * 16
+            lead, rest = split_terms(
+                jnp.concatenate([mid[pl.ds((base + i) * 17, 16), :] for i in range(16)], axis=0)
             )
-            both = dot(row_n, back)
-            for half in range(2):
-                piece = both[:, half * 128 : half * 128 + 128]
-                piece = piece + pltpu.roll(piece, 64, axis=1)
-                piece = jnp.where(lane_low((32, 128)), piece[:32], piece[32:])
-                at = pl.multiple_of((t * 32 + k + half) * 32, 32)
-                back_sum[pl.ds(at, 32), :] += piece.astype(bf16).astype(f32)
-            return row_part + dot(pair_first, back, NT)
-
-        row_part = lax.fori_loop(0, 16, backward, jnp.zeros((64, 128), f32), unroll=4)
+            model = dot(jnp.concatenate([lead, rest], axis=1), to_model, NT)
+
+            def half_of(half):
+                at = (0, pl.ds(base, 16), pl.ds(half * 16, 16), slice(None))
+                data = data_ref[at].reshape(256, 128).astype(f32)
+                weight = weight_ref[at].reshape(256, 128).astype(f32)
+                return (weight * (model[:, half * 128 : half * 128 + 128] - data)).astype(bf16)
+
+            residual = jnp.concatenate([half_of(0), half_of(1)], axis=1)
+            back = dot(residual, to_back)
+            for i in range(16):
+                mid[pl.ds((base + i) * 17, 16), :] = back[i * 16 : i * 16 + 16]
+            return col_part + dot(lead, residual, TN)
+
+        col_part = lax.fori_loop(0, 8, middle, jnp.zeros((128, 256), f32), unroll=MIDDLE)
+        col_sum[q] += (col_part[:64, :128] + col_part[64:, 128:]) * resid_scale
+
+        def backward(kk, row_part):
+            lead, rest = split_terms(mid[pl.ds(kk, 128, stride=17), :])
+            both = dot(row_n2, jnp.concatenate([lead, rest], axis=0))
+            at = pl.ds((t * 16 + kk) * 65, 64)
+            back_sum[at, :] += both.astype(bf16).astype(f32)
+            return row_part + dot(
+                twice(first_ref[t * 16 + kk], 1), jnp.concatenate([lead, rest], axis=1), NT
+            )
+
+        row_part = lax.fori_loop(0, 16, backward, jnp.zeros((64, 128), f32), unroll=BACKWARD)
         rows_out[p] += row_part
 
-    @pl.when(slot == pl.num_programs(0) - 1)
+    @pl.when(slot == last)
     def _():
         cols_out[...] = col_sum[...]
-        slab = slab_ref[...]
-        slab_twice = jnp.concatenate([slab, slab], axis=1)
+        slab_twice = twice(slab_ref[...], 1)
+        core_copy().wait()
 
         def finish(u, depth_part):
-            value = back_sum[pl.ds(u, 128, stride=32), :]
-            lead = value.astype(bf16)
-            rest = (value - lead.astype(f32)).astype(bf16)
+            one = back_sum[pl.ds(u, 64, stride=65), :]
+            two = back_sum[pl.ds(u + 32, 64, stride=65), :]
+            low = low_lanes((64, 128))
+            lead, rest = split_terms(
+                jnp.concatenate(
+                    [
+                        jnp.where(low, one, pltpu.roll(two, 64, axis=1)),
+                        jnp.where(low, pltpu.roll(one, 64, axis=1), two),
+                    ],
+                    axis=0,
+                )
+            )
             core_out[u] = dot(slab_twice, jnp.concatenate([lead, rest], axis=0))
-            piece = jnp.concatenate([core_ref[u], core_ref[u + 32]], axis=0)
-            return depth_part + dot(lead, piece) + dot(rest, piece)
-
-        depth_part = lax.fori_loop(0, 32, finish, jnp.zeros((128, 64), f32), unroll=4)
+            piece = jnp.concatenate([core_in[u], core_in[u + 32]], axis=0)
+            return depth_part + dot(jnp.concatenate([lead, rest], axis=1), twice(piece, 0))
+
+        depth_part = half_inside(
+            lax.fori_loop(0, 32, finish, jnp.zeros((128, 64), f32), unroll=FINISH)
+        )
         depth_out[...] = jnp.concatenate(
             [depth_part, jnp.zeros((128, 64), f32)], axis=1
         ).T[:64]
 
 
+FORWARD, MIDDLE, BACKWARD, FINISH = 4, 2, 4, 4
+
+
 def block_gradients(coords, counts, data, weights, first, rows, cols, slab, core_tensor):
     slots = data.shape[0]
 
     def live(slot, coords, counts):
-        return (jnp.minimum(slot, jnp.maximum(counts[0] - 1, 0)), 0, 0)
+        return (jnp.minimum(slot, jnp.maximum(counts[0, 0, 0] - 1, 0)), 0, 0, 0)
 
     def whole(shape):
         zeros = (0,) * len(shape)
@@ -244,13 +303,13 @@
             num_scalar_prefetch=2,
             grid=(slots,),
             in_specs=[
-                pl.BlockSpec((1, 4096, 128), live),
-                pl.BlockSpec((1, 4096, 128), live),
-                whole((8192, 128)),
-                whole((8, 128, 128)),
-                whole((8, 64, 128)),
+                pl.BlockSpec((1, 128, 32, 128), live),
+                pl.BlockSpec((1, 128, 32, 128), live),
+                whole((64, 64, 128)),
+                whole((8, 8, 8, 128)),
+                whole((8, 32, 128)),
                 whole((64, 128)),
-                whole((64, 64, 64)),
+                pl.BlockSpec(memory_space=pltpu.HBM),
             ],
             out_specs=(
                 whole((32, 64, 128)),
@@ -259,13 +318,15 @@
                 whole((64, 128)),
             ),
             scratch_shapes=[
-                pltpu.VMEM((4096, 128), f32),
-                pltpu.VMEM((4096, 128), f32),
+                pltpu.VMEM((128 * 17, 128), f32),
+                pltpu.VMEM((64 * 65, 128), f32),
                 pltpu.VMEM((4, 64, 128), f32),
+                pltpu.VMEM((64, 64, 64), bf16),
+                pltpu.SemaphoreType.DMA,
             ],
         ),
         compiler_params=pltpu.CompilerParams(
-            dimension_semantics=("arbitrary",), vmem_limit_bytes=48 << 20
+            dimension_semantics=("arbitrary",), vmem_limit_bytes=50331648
         ),
         name="block_gradients",
     )(coords, counts, data, weights, first, rows, cols, slab, core_tensor)
@@ -393,7 +454,7 @@
     row_total = rows_t[pl.ds(pl.multiple_of(z * 16, 16), 16), :]
     for s in range(7):
         row_total = row_total + rows_z[s]
-    rows_out[...] = jnp.concatenate([row_total, jnp.zeros((112, 128), f32)], axis=0).T[:64, :16]
+    rows_out[...] = row_total[:, :64]
 
     own = pl.ds(pl.multiple_of(z * 8, 8), 8)
     arrived(core_z)
@@ -444,7 +505,7 @@
         reduce_kernel,
         out_shape=(
             jax.ShapeDtypeStruct((2, 4, 4, 64, 128), f32),
-            jax.ShapeDtypeStruct((64, 16), f32),
+            jax.ShapeDtypeStruct((16, 64), f32),
             jax.ShapeDtypeStruct((64, 64), f32),
             jax.ShapeDtypeStruct((64, 128), f32),
         ),
@@ -482,21 +543,59 @@
             pltpu.SemaphoreType.DMA((copies,)),
         ],
         compiler_params=pltpu.CompilerParams(
-            collective_id=1, has_side_effects=True, vmem_limit_bytes=32 << 20
+            collective_id=1, has_side_effects=True, vmem_limit_bytes=33554432
         ),
         name="reduce_gradients",
+    )(core, rows, cols, depth)
+
+
+def unpack_kernel(core_ref, rows_ref, cols_ref, depth_ref, core_out, rows_out, cols_out, depth_out):
+    core_out[0] = core_ref[:, :, :64]
+    core_out[1] = core_ref[:, :, 64:]
+
+    @pl.when(pl.program_id(0) == 0)
+    def _():
+        rows_out[...] = rows_ref[...]
+        cols_out[...] = cols_ref[...]
+        depth_out[...] = depth_ref[...]
+
+
+def unpack_results(core, rows, cols, depth):
+    steps = 4
+    part = core.shape[0] // steps
+
+    def whole(value):
+        return pl.BlockSpec(value.shape, lambda step: (0, 0))
+
+    return pl.pallas_call(
+        unpack_kernel,
+        out_shape=(
+            jax.ShapeDtypeStruct((2, 32, 64, 64), f32),
+            jax.ShapeDtypeStruct(rows.shape, f32),
+            jax.ShapeDtypeStruct(cols.shape, f32),
+            jax.ShapeDtypeStruct(depth.shape, f32),
+        ),
+        grid=(steps,),
+        in_specs=[
+            pl.BlockSpec((part, 64, 128), lambda step: (step, 0, 0)),
+            whole(rows), whole(cols), whole(depth),
+        ],
+        out_specs=(
+            pl.BlockSpec((2, part, 64, 64), lambda step: (0, step, 0, 0)),
+            whole(rows), whole(cols), whole(depth),
+        ),
+        compiler_params=pltpu.CompilerParams(dimension_semantics=("arbitrary",), vmem_limit_bytes=8388608),
+        name="unpack_results",
     )(core, rows, cols, depth)
 
 
 def on_device(
     observed, weights, coords, counts, factor_rows, factor_cols, factor_depth, core_tensor
 ):
-    slots = observed.shape[2]
-    data = observed.reshape(slots, 4096, 128)
-    weight = weights.reshape(slots, 4096, 128)
-    rows, cols, slab, first = gather_factors(factor_rows, factor_cols, factor_depth, core_tensor)
+    rows, cols, slab, first = gather_factors(factor_rows.T, factor_cols, factor_depth, core_tensor)
     core_part, rows_part, cols_part, depth_part = block_gradients(
-        coords.reshape(slots * 3), counts.reshape(1), data, weight, first, rows, cols, slab, core_tensor
+        coords, counts, observed.reshape(observed.shape[2:]), weights.reshape(weights.shape[2:]),
+        first, rows, cols, slab, core_tensor,
     )
     core, rows_gradient, cols_gradient, depth_gradient = reduce_gradients(
         core_part.reshape(2, 4, 4, 64, 128),
@@ -504,9 +603,10 @@
         cols_part,
         depth_part.reshape(2, 4, 8, 128),
     )
-    core = core.reshape(32, 64, 128)
-    core_gradient = jnp.concatenate([core[:, :, :64], core[:, :, 64:]], axis=0)
-    return (rows_gradient, cols_gradient, depth_gradient, core_gradient)
+    core, rows_gradient, cols_gradient, depth_gradient = unpack_results(
+        core.reshape(32, 64, 128), rows_gradient, cols_gradient, depth_gradient
+    )
+    return (rows_gradient.T, cols_gradient, depth_gradient, core.reshape(64, 64, 64))
 
 
 def solution(mesh):

time: 106 us -> 86.8 us (0.82)
  Pallas kernels: 94.7 us -> 79.3 us
  local copies, waits for them, and re-layouts: 7.96 us -> 5.52 us
  other arithmetic: 1.49 us -> 0 us
    pallas_call x1, Pallas kernels: 55.9 us -> 47.3 us  [reduce_gradients(): pl.pallas_call(reduce_kernel, out_shape=(jax.ShapeDtypeStruct((2, 4, 4, 6...]
    pallas_call x1, Pallas kernels: 19.3 us -> 12.7 us  [block_gradients(): pl.pallas_call(block_kernel, out_shape=(jax.ShapeDtypeStruct((32, 64, 128...]
    unnamed x13 -> x11, local copies, waits for them, and re-layouts: 7.51 us -> 5.52 us
    concatenate x1 -> x0, other arithmetic: 1.49 us -> none  [on_device(): core_gradient = jnp.concatenate([core[:, :, :64], core[:, :, 64:]], axis=0)]
    pallas_call x1 -> x2, Pallas kernels: 19.5 us -> 19.3 us  [the longest x1 17.2 us: gather_factors(): pl.pallas_call(gather_kernel, out_shape=(jax.ShapeDtypeStruct((8, 8, 8, 1...]
where the time goes in v2:
time: 86.8 us; the launch traced here: 86.2 us
  Pallas kernels  79.3 us (91%)
  local copies, waits for them, and re-layouts  5.52 us (6%)
  between operations  1.31 us (2%)
    pallas_call x1, Pallas kernels, reduce_gradients(): pl.pallas_call(reduce_kernel, out_shape=(jax.ShapeDtypeStruct((2, 4, 4, 6...  47.3 us
    pallas_call x1, Pallas kernels, gather_factors(): pl.pallas_call(gather_kernel, out_shape=(jax.ShapeDtypeStruct((8, 8, 8, 1...  17.2 us
    pallas_call x1, Pallas kernels, block_gradients(): pl.pallas_call(block_kernel, out_shape=(jax.ShapeDtypeStruct((32, 64, 128...  12.7 us
    unnamed x11, local copies, waits for them, and re-layouts  5.52 us
    pallas_call x1, Pallas kernels, unpack_results(): pl.pallas_call(unpack_kernel, out_shape=(jax.ShapeDtypeStruct((2, 32, 64,...  2.08 us

profile of v2, /device:TPU:1, one launch (start us, length us, event | category | flops | bytes accessed | tf_op | source)
XLA Modules:
  0.0 86.2 jit_solution(9849137514468391807)
XLA Ops:
  1.3 0.8 copy.12.coords
  2.0 0.0 copy-start
  2.0 1.2 %copy-done = bf16[64,64,64]{2,1,0:T(8,128)(2,1)S(1)} copy-done((bf16[64,64,64]{2,1,0:T(8,128)(2,1)S(1)}, bf16[64,64,64]{2,1,0:T(8,128)(2,1)}, u32[]{:S(2)}) %copy-start) | copy-done | bytes 524312
  3.3 0.0 copy-start.2
  3.3 0.9 %copy-done.2 = bf16[64,1024]{1,0:T(8,128)(2,1)S(1)} copy-done((bf16[64,1024]{1,0:T(8,128)(2,1)S(1)}, bf16[64,1024]{1,0:T(8,128)(2,1)}, u32[]{:S(2)}) %copy-start.2) | copy-done | bytes 131096
  4.2 0.0 copy-start.3
  4.2 0.7 copy-done.3
  4.9 0.0 copy-start.4
  4.9 0.7 copy-done.4
  5.6 17.2 %gather_factors.1 = (bf16[8,8,8,128]{3,2,1,0:T(8,128)(2,1)S(1)}, bf16[8,32,128]{2,1,0:T(8,128)(2,1)S(1)}, bf16[64,128]{1,0:T(8,128)(2,1)S(1)}, bf16[64,64,128]{2,1,0:T(8,128)(2,1)S(1)}) custom-call(bf16[16,64]{1,0:T(8,128)(2,1)S(1)} %bitcast.13, bf16[64,64]{1,0:T(8,128)(2,1)S(1)} %copy-done.3, bf16[64,1024]{1,0:T(8,128)(2,1)S(1)} %copy-done.2, ...), custom_call_target="tpu_custom_call" | custom-call | tf_op jit(solution)/shard_map/gather_factors/pallas_call | solution.py:132
  22.8 0.0 copy-start.1
  22.8 1.2 %copy-done.1 = bf16[64,64,64]{2,1,0:T(8,128)(2,1)S(1)} copy-done((bf16[64,64,64]{2,1,0:T(8,128)(2,1)S(1)}, bf16[64,64,64]{2,1,0:T(8,128)(2,1)}, u32[]{:S(2)}) %copy-start.1) | copy-done | bytes 524312
  24.0 12.7 %block_gradients.1 = (f32[32,64,128]{2,1,0:T(8,128)S(1)}, f32[8,64,128]{2,1,0:T(8,128)S(1)}, f32[4,64,128]{2,1,0:T(8,128)S(1)}, f32[64,128]{1,0:T(8,128)S(1)}) custom-call(s32[1,1,5,3]{3,2,1,0:T(8,128)S(1)} %copy.12.coords, s32[1,1,1]{2,1,0:T(1,128)S(6)} %copy.13.counts, bf16[5,128,32,128]{3,2,1,0:T(8,128)(2,1)} %bitcast.14, ...), custom_call_target="tpu_custom_call" | custom-call | tf_op jit(solution)/shard_map/block_gradients/pallas_call | solution.py:294
  36.8 47.3 %reduce_gradients.1 = (f32[2,4,4,64,128]{4,3,2,1,0:T(8,128)S(1)}, f32[16,64]{1,0:T(8,128)S(1)}, f32[64,64]{1,0:T(8,128)S(1)}, f32[64,128]{1,0:T(8,128)S(1)}) custom-call(f32[2,4,4,64,128]{4,3,2,1,0:T(8,128)S(1)} %bitcast.9, f32[4,2,64,128]{3,2,1,0:T(8,128)S(1)} %bitcast.11, f32[4,64,128]{2,1,0:T(8,128)S(1)} %get-tuple-element.26.cols_ref, ...), custom_call_target="tpu_custom_call" | custom-call | tf_op jit(solution)/shard_map/reduce_gradients/pallas_call | solution.py:504
  84.1 2.1 %unpack_results.1 = (f32[2,32,64,64]{3,2,1,0:T(8,128)}, f32[16,64]{1,0:T(8,128)}, f32[64,64]{1,0:T(8,128)}, f32[64,128]{1,0:T(8,128)}) custom-call(f32[32,64,128]{2,1,0:T(8,128)S(1)} %bitcast.10, f32[16,64]{1,0:T(8,128)S(1)} %get-tuple-element.29.rows_ref, f32[64,64]{1,0:T(8,128)S(1)} %get-tuple-element.30.cols_ref, f32[64,128]{1,0:T(8,128)S(1)} %get-tuple-element.31.depth_ref), custom_call_target="tpu_custom_call" | custom-call | tf_op jit(solution)/shard_map/unpack_results/pallas_call | solution.py:570
Async XLA Ops:
  2.0 1.2 %copy-start = (bf16[64,64,64]{2,1,0:T(8,128)(2,1)S(1)}, bf16[64,64,64]{2,1,0:T(8,128)(2,1)}, u32[]{:S(2)}) copy-start(bf16[64,64,64]{2,1,0:T(8,128)(2,1)} %core_hbm.3) | copy-start | bytes 1572868
  3.3 0.9 %copy-start.2 = (bf16[64,1024]{1,0:T(8,128)(2,1)S(1)}, bf16[64,1024]{1,0:T(8,128)(2,1)}, u32[]{:S(2)}) copy-start(bf16[64,1024]{1,0:T(8,128)(2,1)} %depth_hbm.1) | copy-start | bytes 393220
  4.2 0.7 copy-start.3
  4.9 0.7 copy-start.4
  22.8 1.2 %copy-start.1 = (bf16[64,64,64]{2,1,0:T(8,128)(2,1)S(1)}, bf16[64,64,64]{2,1,0:T(8,128)(2,1)}, u32[]{:S(2)}) copy-start(bf16[64,64,64]{2,1,0:T(8,128)(2,1)} %core_hbm.3) | copy-start | bytes 1572868

commit v3 on v2

v3 whole, which is shorter than its diff:
```python
import jax
import jax.numpy as jnp
from jax import lax
from jax.experimental import pallas as pl
from jax.experimental.pallas import tpu as pltpu
from jax.sharding import PartitionSpec as P

MESH = pl.DeviceIdType.MESH
f32 = jnp.float32
bf16 = jnp.bfloat16
resid_scale = 1.0 / 64.0

NN = (((1,), (0,)), ((), ()))
NT = (((1,), (1,)), ((), ()))
TN = (((0,), (0,)), ((), ()))


def dot(a, b, dims=NN):
    return lax.dot_general(a, b, dims, preferred_element_type=f32)


def low_lanes(shape):
    return lax.broadcasted_iota(jnp.int32, shape, len(shape) - 1) < 64


def unit(size):
    return (
        lax.broadcasted_iota(jnp.int32, (size, size), 0)
        == lax.broadcasted_iota(jnp.int32, (size, size), 1)
    ).astype(bf16)


def twice(value, axis):
    return jnp.concatenate([value, value], axis=axis)


def same(a, b):
    return (1 - jnp.minimum((a - b) * (a - b), 1)).astype(f32)


def split_terms(value):
    lead = value.astype(bf16)
    return lead, (value - lead.astype(f32)).astype(bf16)


def tucker_kernel(
    coords, counts, rows_hbm, cols_hbm, depth_hbm, core_hbm, data_hbm, weight_hbm,
    core_out, rows_out, cols_out, depth_out,
    rows_in, cols_in, slab_in, core_in, data_in, weight_in,
    row_buf, col_buf, slab_buf, first_wide, first_buf, mid, back_buf, core_own, rows_own_sum, cols_own_sum, depth_own,
    core_pair, core_sum, core_x, core_y, half_x, half_y, end_y, end_x, tile_sum, tile_in, tile_all, core_all,
    rows_pair, rows_sum, rows_x, rows_t, rows_z,
    cols_y, cols_sum, cols_z, cols_all,
    depth_pair, depth_sum, depth_x, depth_one, depth_y, depth_all,
    send_sem, recv_sem, local_sem, data_sem, weight_sem,
):
    y = lax.axis_index("ia")
    ja = lax.axis_index("ja")
    z = lax.axis_index("ka")
    x = ja // 2
    c = ja % 2
    o = 1 - c
    low = pl.ds(0, 32)
    high = pl.ds(32, 32)

    def fetch(src, dst, sem):
        copy = pltpu.make_async_copy(src, dst, sem)
        copy.start()
        return copy

    rows_copy = fetch(rows_hbm, rows_in, local_sem.at[0])
    cols_copy = fetch(cols_hbm, cols_in, local_sem.at[1])
    slab_copy = fetch(
        depth_hbm.at[:, pl.ds(pl.multiple_of(z * 128, 128), 128)], slab_in, local_sem.at[2]
    )
    core_copy = fetch(core_hbm, core_in, local_sem.at[3])

    def mate():
        return {"ja": x * 2 + o}

    def on_ja(step):
        return {"ja": (ja + step) % 8}

    def on_x(step):
        return {"ja": ((x + step) % 4) * 2 + c}

    def on_y(step):
        return {"ia": (y + step) % 4}

    def on_z(step):
        return {"ka": (z + step) % 8}

    barrier = pltpu.get_barrier_semaphore()
    targets = [on_z(s) for s in range(1, 8)] + [on_ja(s) for s in range(1, 8)] + [on_y(s) for s in (1, 2, 3)]
    for target in targets:
        pl.semaphore_signal(barrier, inc=1, device_id=target, device_id_type=MESH)

    slots = data_hbm.shape[0]
    for slot in range(slots):
        fetch(data_hbm.at[slot], data_in.at[slot], data_sem.at[slot])
        fetch(weight_hbm.at[slot], weight_in.at[slot], weight_sem.at[slot])

    started = []

    def send(src, dst, target):
        slot = len(started)
        copy = pltpu.make_async_remote_copy(
            src_ref=src, dst_ref=dst, send_sem=send_sem.at[slot], recv_sem=recv_sem.at[slot],
            device_id=target, device_id_type=MESH,
        )
        copy.start()
        started.append(copy)
        return copy

    def arrived(copies):
        for copy in copies:
            copy.wait_recv()

    rows_copy.wait()
    own_rows = dot(rows_in[...], twice(unit(64), 1))
    row_buf[ja, z] = jnp.where(low_lanes((8, 128)), own_rows[:8], own_rows[8:]).astype(bf16)
    cols_copy.wait()
    own_cols = dot(unit(64), twice(cols_in[...], 0), NT)
    col_buf[z] = jnp.where(low_lanes((32, 128)), own_cols[:32], own_cols[32:]).astype(bf16)
    pl.semaphore_wait(barrier, len(targets))
    order = (4, 3, 5, 2, 6, 1, 7)
    deep_rows = [send(row_buf.at[ja, z], row_buf.at[ja, z], on_z(s)) for s in order]
    deep_cols = [send(col_buf.at[z], col_buf.at[z], on_z(s)) for s in order]

    slab_copy.wait()
    slab_turned = dot(unit(128), slab_in[...], NT)
    slab_buf[...] = slab_turned.reshape(8, 16, 64)
    slab_rows = jnp.concatenate(
        [slab_turned[t * 32 + half * 16 : t * 32 + half * 16 + 16] for half in range(2) for t in range(4)], axis=0
    ).astype(bf16)
    core_copy.wait()

    def first_of(pair, carry):
        left = core_in[pair * 2]
        right = core_in[pair * 2 + 1]
        both = dot(slab_rows, jnp.concatenate([left, left, right, right], axis=0), NT)
        for side in range(2):
            piece = both[:, side * 128 : side * 128 + 128]
            first_wide[pl.ds(pair * 2 + side, 64, stride=65), :] = jnp.where(
                low_lanes((64, 128)), piece[:64], piece[64:]
            )
        return carry

    lax.fori_loop(0, 32, first_of, 0, unroll=4)

    arrived(deep_rows)
    wide_rows = [send(row_buf.at[ja], row_buf.at[ja], on_ja(s)) for s in order]

    def round_of(step, carry):
        first_buf[step] = first_wide[pl.ds(step * 65, 64), :].astype(bf16)
        return carry

    lax.fori_loop(0, 64, round_of, 0, unroll=8)
    rows_own_sum[...] = jnp.zeros_like(rows_own_sum)
    cols_own_sum[...] = jnp.zeros_like(cols_own_sum)
    arrived(deep_cols)
    arrived(wide_rows)

    live_count = counts[0, 0, 0]

    def place(slot):
        p = coords[0, 0, 0, slot] & 7
        q = coords[0, 1, 0, slot] & 3
        t = coords[0, 2, 0, slot] & 3
        return p, q, t

    def one_slot(slot, carry):
        p, q, t = place(slot)
        alive = jnp.clip(live_count - slot, 0, 1).astype(f32)
        packed_rows = row_buf[p].astype(f32).reshape(64, 128)
        turned_rows = pltpu.roll(packed_rows, 64, axis=1)
        row_t = jnp.concatenate(
            [part[s * 8 : s * 8 + 8] for s in range(8) for part in (packed_rows, turned_rows)], axis=0
        )[:, :64].astype(bf16)
        row_n = (dot(unit(64), row_t, NT) * alive).astype(bf16)
        row_n2 = twice(row_n, 1)
        packed_cols = jnp.concatenate([col_buf[q * 2], col_buf[q * 2 + 1]], axis=0).astype(f32)
        turned_cols = pltpu.roll(packed_cols, 64, axis=1)
        left = low_lanes((64, 128))
        first_half = jnp.where(left, packed_cols, turned_cols)
        second_half = jnp.where(left, turned_cols, packed_cols)
        col_t = jnp.concatenate(
            [first_half[:32], second_half[:32], first_half[32:], second_half[32:]], axis=0
        )
        left = low_lanes((128, 128))
        zero = jnp.zeros((128, 128), f32)
        col_low = jnp.where(left, col_t, zero)
        col_high = jnp.where(left, zero, col_t)
        to_model = jnp.concatenate([twice(col_low, 1), twice(col_high, 1)], axis=0).astype(bf16)
        to_back = (jnp.concatenate([col_low, col_high], axis=0) * resid_scale).astype(bf16)

        def forward(pair, carry):
            kk = pair * 2
            part = dot(
                row_t, jnp.concatenate([first_buf[t * 16 + kk], first_buf[t * 16 + kk + 1]], axis=1)
            )
            mid[pl.ds(kk, 128, stride=17), :] = part[:, :128]
            mid[pl.ds(kk + 1, 128, stride=17), :] = part[:, 128:]
            return carry

        lax.fori_loop(0, 8, forward, 0, unroll=8)
        pltpu.make_async_copy(data_hbm.at[slot], data_in.at[slot], data_sem.at[slot]).wait()
        pltpu.make_async_copy(weight_hbm.at[slot], weight_in.at[slot], weight_sem.at[slot]).wait()

        def middle(step, col_part):
            base = step * 16
            lead, rest = split_terms(
                jnp.concatenate([mid[pl.ds((base + i) * 17, 16), :] for i in range(16)], axis=0)
            )
            model = dot(jnp.concatenate([lead, rest], axis=1), to_model, NT)

            def half_of(half):
                at = (slot, pl.ds(base, 16), pl.ds(half * 16, 16), slice(None))
                data = data_in[at].reshape(256, 128).astype(f32)
                weight = weight_in[at].reshape(256, 128).astype(f32)
                return (weight * (model[:, half * 128 : half * 128 + 128] - data)).astype(bf16)

            residual = jnp.concatenate([half_of(0), half_of(1)], axis=1)
            back = dot(residual, to_back)
            for i in range(16):
                mid[pl.ds((base + i) * 17, 16), :] = back[i * 16 : i * 16 + 16]
            return col_part + dot(lead, residual, TN)

        col_part = lax.fori_loop(0, 8, middle, jnp.zeros((128, 256), f32), unroll=MIDDLE)
        col_part = (col_part[:64, :128] + col_part[64:, 128:]) * resid_scale
        for part in range(4):
            cols_own_sum[part] += col_part * (same(q, part) * alive)

        def backward(kk, row_part):
            lead, rest = split_terms(mid[pl.ds(kk, 128, stride=17), :])
            both = dot(row_n2, jnp.concatenate([lead, rest], axis=0))
            back_buf[pl.ds((slot * 16 + kk) * 65, 64), :] = both.astype(bf16).astype(f32)
            return row_part + dot(
                twice(first_buf[t * 16 + kk], 1), jnp.concatenate([lead, rest], axis=1), NT
            )

        row_part = lax.fori_loop(0, 16, backward, jnp.zeros((64, 128), f32), unroll=16)
        for part in range(8):
            rows_own_sum[part // 2, part % 2] += row_part * (same(p, part) * alive)
        return carry

    lax.fori_loop(0, slots, one_slot, 0)

    rows_c = send(rows_own_sum.at[:, o], rows_pair, mate())
    cols_s1 = [
        send(cols_own_sum.at[:, pl.ds(pl.multiple_of(((y + s) % 4) * 16, 16), 16), :], cols_y.at[s - 1], on_y(s))
        for s in (1, 2, 3)
    ]

    slab_slots = jnp.concatenate(
        [
            slab_buf[place(slot)[2] * 2 + half]
            for half in range(2)
            for slot in range(slots)
        ],
        axis=0,
    ).astype(bf16)
    slab_n = dot(unit(64), slab_slots, NT).astype(bf16)
    tall = slots * 16
    left_tall = low_lanes((tall, 128))

    def finish_group(half, group, depth_part):
        def finish(step, depth_part):
            u = half * 16 + group * 4 + step
            one = back_buf[pl.ds(u, tall, stride=65), :]
            two = back_buf[pl.ds(u + 32, tall, stride=65), :]
            both = jnp.concatenate(
                [
                    jnp.where(left_tall, one, pltpu.roll(two, 64, axis=1)),
                    jnp.where(left_tall, pltpu.roll(one, 64, axis=1), two),
                ],
                axis=0,
            ).astype(bf16)
            core_own[half, group, step] = dot(slab_n, both)
            piece = jnp.concatenate([core_in[u], core_in[u + 32]], axis=0)
            return depth_part + dot(both, piece)

        return lax.fori_loop(0, 4, finish, depth_part, unroll=4)

    depth_part = jnp.zeros((2 * tall, 64), f32)
    core_c = []
    for group in range(4):
        depth_part = finish_group(o, group, depth_part)
        core_c.append(send(core_own.at[o, group], core_pair.at[group], mate()))
    rows_c.wait_recv()
    rows_sum[...] = rows_own_sum[:, c] + rows_pair[...]
    rows_s1 = [send(rows_sum.at[(x + s) % 4], rows_x.at[s - 1], on_x(s)) for s in (1, 2, 3)]
    for group in range(4):
        depth_part = finish_group(c, group, depth_part)

    depth_pieces = []
    for t in range(4):
        for half in range(2):
            piece = jnp.zeros((16, 64), f32)
            for slot in range(slots):
                at = half * tall + slot * 16
                piece = piece + depth_part[at : at + 16] * same(place(slot)[2], t)
            depth_pieces.append(piece)
    depth_turned = jnp.concatenate(
        [jnp.concatenate(depth_pieces, axis=0), jnp.zeros((128, 64), f32)], axis=1
    ).T[:64]
    depth_own[...] = depth_turned.reshape(2, 4, 8, 128)
    depth_c = send(depth_own.at[o], depth_pair, mate())

    core_x0 = []
    for group in range(4):
        core_c[group].wait_recv()
        core_sum[group] = core_own[c, group] + core_pair[group]
    core_x0 = [send(core_sum.at[(x + s) % 4, :, low], core_x.at[s - 1], on_x(s)) for s in (2, 1, 3)]
    core_y1 = [send(core_sum.at[:, (y + s) % 4, high], core_y.at[s - 1], on_y(s)) for s in (2, 1, 3)]
    depth_c.wait_recv()
    depth_sum[...] = depth_own[c] + depth_pair[...]
    depth_s1 = [send(depth_sum.at[(x + s) % 4], depth_x.at[s - 1], on_x(s)) for s in (1, 2, 3)]

    arrived(cols_s1)
    cols_sum[...] = (
        cols_own_sum[:, pl.ds(pl.multiple_of(y * 16, 16), 16), :] + cols_y[0] + cols_y[1] + cols_y[2]
    )
    cols_s2 = [send(cols_sum.at[((z + s) % 8) // 2], cols_z.at[s - 1], on_z(s)) for s in range(1, 8)]

    arrived(core_x0)
    half_x[...] = core_sum[x, :, low] + core_x[0] + core_x[1] + core_x[2]
    core_y0 = [send(half_x.at[(y + s) % 4], end_y.at[s - 1], on_y(s)) for s in (1, 2, 3)]
    arrived(core_y1)
    half_y[...] = core_sum[:, y, high] + core_y[0] + core_y[1] + core_y[2]
    core_x1 = [send(half_y.at[(x + s) % 4], end_x.at[s - 1], on_x(s)) for s in (1, 2, 3)]

    arrived(rows_s1)
    rows_own = rows_sum[x] + rows_x[0] + rows_x[1] + rows_x[2]
    rows_t[...] = jnp.concatenate([rows_own, jnp.zeros((64, 128), f32)], axis=0).T
    rows_s2 = [
        send(rows_t.at[pl.ds(pl.multiple_of(((z + s) % 8) * 16, 16), 16), :], rows_z.at[s - 1], on_z(s))
        for s in range(1, 8)
    ]
    arrived(depth_s1)
    depth_one[...] = depth_sum[x] + depth_x[0] + depth_x[1] + depth_x[2]
    depth_s2 = [send(depth_one, depth_y.at[s - 1], on_y(s)) for s in (1, 2, 3)]

    arrived(core_y0)
    tile_sum[low] = half_x[y] + end_y[0] + end_y[1] + end_y[2]
    arrived(core_x1)
    tile_sum[high] = half_y[x] + end_x[0] + end_x[1] + end_x[2]
    core_z = [
        send(tile_sum.at[pl.ds(pl.multiple_of(((z + s) % 8) * 8, 8), 8), :], tile_in.at[s - 1], on_z(s))
        for s in range(1, 8)
    ]

    arrived(cols_s2)
    col_total = cols_sum[z // 2]
    for s in range(7):
        col_total = col_total + cols_z[s]
    cols_all[y] = col_total
    cols_s3 = [send(cols_all.at[y], cols_all.at[y], on_y(s)) for s in (1, 2, 3)]
    arrived(depth_s2)
    depth_all[c, x] = depth_one[...] + depth_y[0] + depth_y[1] + depth_y[2]
    depth_s3 = [send(depth_all.at[c, x], depth_all.at[c, x], on_x(s)) for s in (1, 2, 3)]
    arrived(rows_s2)
    row_total = rows_t[pl.ds(pl.multiple_of(z * 16, 16), 16), :]
    for s in range(7):
        row_total = row_total + rows_z[s]
    rows_out[...] = row_total[:, :64]

    own = pl.ds(pl.multiple_of(z * 8, 8), 8)
    arrived(core_z)
    total = tile_sum[own, :]
    for s in range(7):
        total = total + tile_in[s]
    tile_all[own, :] = total
    core_g = [send(tile_all.at[own, :], tile_all.at[own, :], on_z(s)) for s in range(1, 8)]
    arrived(depth_s3)
    depth_s4 = send(depth_all.at[c], depth_all.at[c], mate())
    arrived(core_g)
    turned = jnp.concatenate([tile_all[...], jnp.zeros((64, 128), f32)], axis=0).T
    core_all[c, x, y] = turned[:64] + pltpu.roll(turned[64:], 64, axis=1)

    back_y0 = [send(core_all.at[c, x, y, low], core_all.at[c, x, y, low], on_y(s)) for s in (1, 2, 3)]
    back_x1 = [send(core_all.at[c, x, y, high], core_all.at[c, x, y, high], on_x(s)) for s in (1, 2, 3)]
    arrived(back_y0)
    back_x0 = [send(core_all.at[c, x, :, low], core_all.at[c, x, :, low], on_x(s)) for s in (1, 2, 3)]
    arrived(back_x1)
    back_y1 = [send(core_all.at[c, :, y, high], core_all.at[c, :, y, high], on_y(s)) for s in (1, 2, 3)]

    arrived(cols_s3)
    whole = cols_all[...].reshape(64, 128)
    cols_out[...] = jnp.where(z % 2 == 1, pltpu.roll(whole, 64, axis=1), whole)[:, :64]

    arrived(back_x0)
    back_c0 = send(core_all.at[c, :, :, low], core_all.at[c, :, :, low], mate())
    arrived(back_y1)
    back_c1 = send(core_all.at[c, :, :, high], core_all.at[c, :, :, high], mate())
    depth_s4.wait_recv()
    depth_out[...] = depth_all[...].reshape(64, 128)
    own_half = fetch(core_all.at[c], core_out.at[c], local_sem.at[4])
    back_c0.wait_recv()
    back_c1.wait_recv()
    other_half = fetch(core_all.at[o], core_out.at[o], local_sem.at[5])
    for copy in started:
        copy.wait_send()
    own_half.wait()
    other_half.wait()


MIDDLE = 4


def tucker_gradients(coords, counts, rows, cols, depth, core, data, weights):
    vmem = pl.BlockSpec(memory_space=pltpu.VMEM)
    smem = pl.BlockSpec(memory_space=pltpu.SMEM)
    hbm = pl.BlockSpec(memory_space=pltpu.HBM)
    slots = data.shape[0]
    copies = 110

    def buf(*shape):
        return pltpu.VMEM(shape, f32)

    def buf16(*shape):
        return pltpu.VMEM(shape, bf16)

    return pl.pallas_call(
        tucker_kernel,
        out_shape=(
            jax.ShapeDtypeStruct((2, 4, 4, 64, 128), f32),
            jax.ShapeDtypeStruct((16, 64), f32),
            jax.ShapeDtypeStruct((64, 64), f32),
            jax.ShapeDtypeStruct((64, 128), f32),
        ),
        in_specs=[smem, smem] + [hbm] * 6,
        out_specs=(hbm, vmem, vmem, vmem),
        scratch_shapes=[
            buf16(16, 64),
            buf16(64, 64),
            buf16(64, 128),
            buf16(64, 64, 64),
            buf16(slots, 128, 32, 128),
            buf16(slots, 128, 32, 128),
            buf16(8, 8, 8, 128),
            buf16(8, 32, 128),
            buf(8, 16, 64),
            buf(64 * 65, 128),
            buf16(64, 64, 128),
            buf(128 * 17, 128),
            buf(slots * 16 * 65, 128),
            buf(2, 4, 4, 64, 128),
            buf(4, 2, 64, 128),
            buf(4, 64, 128),
            buf(2, 4, 8, 128),
            buf(4, 4, 64, 128),
            buf(4, 4, 64, 128),
            buf(3, 4, 32, 128),
            buf(3, 4, 32, 128),
            buf(4, 32, 128),
            buf(4, 32, 128),
            buf(3, 32, 128),
            buf(3, 32, 128),
            buf(64, 128),
            buf(7, 8, 128),
            buf(64, 128),
            buf(2, 4, 4, 64, 128),
            buf(4, 64, 128),
            buf(4, 64, 128),
            buf(3, 64, 128),
            buf(128, 128),
            buf(7, 16, 128),
            buf(3, 4, 16, 128),
            buf(4, 16, 128),
            buf(7, 16, 128),
            buf(4, 16, 128),
            buf(4, 8, 128),
            buf(4, 8, 128),
            buf(3, 8, 128),
            buf(8, 128),
            buf(3, 8, 128),
            buf(2, 4, 8, 128),
            pltpu.SemaphoreType.DMA((copies,)),
            pltpu.SemaphoreType.DMA((copies,)),
            pltpu.SemaphoreType.DMA((6,)),
            pltpu.SemaphoreType.DMA((slots,)),
            pltpu.SemaphoreType.DMA((slots,)),
        ],
        compiler_params=pltpu.CompilerParams(
            collective_id=0, has_side_effects=True, vmem_limit_bytes=67043328
        ),
        name="tucker_gradients",
    )(coords, counts, rows, cols, depth, core, data, weights)


def unpack_kernel(core_ref, rows_ref, cols_ref, depth_ref, core_out, rows_out, cols_out, depth_out):
    core_out[0] = core_ref[:, :, :64]
    core_out[1] = core_ref[:, :, 64:]

    @pl.when(pl.program_id(0) == 0)
    def _():
        rows_out[...] = rows_ref[...]
        cols_out[...] = cols_ref[...]
        depth_out[...] = depth_ref[...]


def unpack_results(core, rows, cols, depth):
    steps = 4
    part = core.shape[0] // steps

    def whole(value):
        return pl.BlockSpec(value.shape, lambda step: (0, 0))

    return pl.pallas_call(
        unpack_kernel,
        out_shape=(
            jax.ShapeDtypeStruct((2, 32, 64, 64), f32),
            jax.ShapeDtypeStruct(rows.shape, f32),
            jax.ShapeDtypeStruct(cols.shape, f32),
            jax.ShapeDtypeStruct(depth.shape, f32),
        ),
        grid=(steps,),
        in_specs=[
            pl.BlockSpec((part, 64, 128), lambda step: (step, 0, 0)),
            whole(rows), whole(cols), whole(depth),
        ],
        out_specs=(
            pl.BlockSpec((2, part, 64, 64), lambda step: (0, step, 0, 0)),
            whole(rows), whole(cols), whole(depth),
        ),
        compiler_params=pltpu.CompilerParams(dimension_semantics=("arbitrary",), vmem_limit_bytes=67043328),
        name="unpack_results",
    )(core, rows, cols, depth)


def on_device(
    observed, weights, coords, counts, factor_rows, factor_cols, factor_depth, core_tensor
):
    core, rows_gradient, cols_gradient, depth_gradient = tucker_gradients(
        coords.transpose(0, 3, 1, 2), counts, factor_rows.T, factor_cols, factor_depth, core_tensor,
        observed.reshape(observed.shape[2:]), weights.reshape(weights.shape[2:]),
    )
    core, rows_gradient, cols_gradient, depth_gradient = unpack_results(
        core.reshape(32, 64, 128), rows_gradient, cols_gradient, depth_gradient
    )
    return (rows_gradient.T, cols_gradient, depth_gradient, core.reshape(64, 64, 64))


def solution(mesh):
    in_specs = (
        P("ia", "ja", "ka", None, None, None),
        P("ia", "ja", "ka", None, None, None),
        P("ia", "ja", "ka", None),
        P("ia", "ja", "ka"),
        P(None, ("ia", "ja", "ka")),
        P(None, ("ja", "ka")),
        P(),
        P(),
    )
    out_specs = (P(None, ("ia", "ja", "ka")), P(None, ("ja", "ka")), P(None, "ka"), P())
    return jax.shard_map(
        on_device, mesh=mesh, in_specs=in_specs, out_specs=out_specs, check_vma=False
    )
```

time: 86.8 us -> 71.7 us (0.83)
  Pallas kernels: 79.3 us -> 70.2 us
  local copies, waits for them, and re-layouts: 5.52 us -> 0 us
    pallas_call x3 -> x1, Pallas kernels: 77.2 us -> 66.4 us  [tucker_gradients(): pl.pallas_call(tucker_kernel, out_shape=(jax.ShapeDtypeStruct((2, 4, 4, 6...]
    unnamed x11 -> x0, local copies, waits for them, and re-layouts: 5.52 us -> none
    pallas_call x1, Pallas kernels: 2.08 us -> 3.82 us  [unpack_results(): pl.pallas_call(unpack_kernel, out_shape=(jax.ShapeDtypeStruct((2, 32, 64,...]
where the time goes in v3:
time: 71.7 us; the launch traced here: 71.5 us
  Pallas kernels  70.2 us (98%)
  between operations  1.29 us (2%)
    pallas_call x1, Pallas kernels, tucker_gradients(): pl.pallas_call(tucker_kernel, out_shape=(jax.ShapeDtypeStruct((2, 4, 4, 6...  66.4 us
    pallas_call x1, Pallas kernels, unpack_results(): pl.pallas_call(unpack_kernel, out_shape=(jax.ShapeDtypeStruct((2, 32, 64,...  3.82 us

profile of v3, /device:TPU:1, one launch (start us, length us, event | category | flops | bytes accessed | tf_op | source)
XLA Modules:
  0.0 71.5 jit_solution(4080092401875249401)
XLA Ops:
  1.3 66.4 %tucker_gradients.1 = (f32[2,4,4,64,128]{4,3,2,1,0:T(8,128)}, f32[16,64]{1,0:T(8,128)}, f32[64,64]{1,0:T(8,128)}, f32[64,128]{1,0:T(8,128)}) custom-call(s32[1,3,1,5]{3,2,1,0:T(1,128)} %bitcast.11, s32[1,1,1]{2,1,0:T(1,128)S(6)} %copy.12.counts, bf16[16,64]{1,0:T(8,128)(2,1)} %bitcast.10, bf16[64,64]{1,0:T(8,128)(2,1)} %cols_hbm.1, ...), custom_call_target="tpu_custom_call" | custom-call | tf_op jit(solution)/shard_map/tucker_gradients/pallas_call | solution.py:424
  67.7 3.8 %unpack_results.1 = (f32[2,32,64,64]{3,2,1,0:T(8,128)}, f32[16,64]{1,0:T(8,128)}, f32[64,64]{1,0:T(8,128)}, f32[64,128]{1,0:T(8,128)}) custom-call(f32[32,64,128]{2,1,0:T(8,128)} %bitcast.9, f32[16,64]{1,0:T(8,128)} %get-tuple-element.13.rows_ref, f32[64,64]{1,0:T(8,128)} %get-tuple-element.14.cols_ref, f32[64,128]{1,0:T(8,128)} %get-tuple-element.15.depth_ref), custom_call_target="tpu_custom_call" | custom-call | tf_op jit(solution)/shard_map/unpack_results/pallas_call | solution.py:510

commit v4 on v3

--- a/solution.py
+++ b/solution.py
@@ -307,12 +307,20 @@
     depth_own[...] = depth_turned.reshape(2, 4, 8, 128)
     depth_c = send(depth_own.at[o], depth_pair, mate())
 
-    core_x0 = []
     for group in range(4):
         core_c[group].wait_recv()
         core_sum[group] = core_own[c, group] + core_pair[group]
-    core_x0 = [send(core_sum.at[(x + s) % 4, :, low], core_x.at[s - 1], on_x(s)) for s in (2, 1, 3)]
-    core_y1 = [send(core_sum.at[:, (y + s) % 4, high], core_y.at[s - 1], on_y(s)) for s in (2, 1, 3)]
+    far_first = (2, 1, 3)
+    core_x0, core_y1 = {}, {}
+    for other in (2, 1, 3, 0):
+        at_y = (y + other) % 4
+        at_x = (x + other) % 4
+        core_x0[other] = [
+            send(core_sum.at[(x + s) % 4, at_y, low], core_x.at[s - 1, at_y], on_x(s)) for s in far_first
+        ]
+        core_y1[other] = [
+            send(core_sum.at[at_x, (y + s) % 4, high], core_y.at[s - 1, at_x], on_y(s)) for s in far_first
+        ]
     depth_c.wait_recv()
     depth_sum[...] = depth_own[c] + depth_pair[...]
     depth_s1 = [send(depth_sum.at[(x + s) % 4], depth_x.at[s - 1], on_x(s)) for s in (1, 2, 3)]
@@ -323,12 +331,18 @@
     )
     cols_s2 = [send(cols_sum.at[((z + s) % 8) // 2], cols_z.at[s - 1], on_z(s)) for s in range(1, 8)]
 
-    arrived(core_x0)
-    half_x[...] = core_sum[x, :, low] + core_x[0] + core_x[1] + core_x[2]
-    core_y0 = [send(half_x.at[(y + s) % 4], end_y.at[s - 1], on_y(s)) for s in (1, 2, 3)]
-    arrived(core_y1)
-    half_y[...] = core_sum[:, y, high] + core_y[0] + core_y[1] + core_y[2]
-    core_x1 = [send(half_y.at[(x + s) % 4], end_x.at[s - 1], on_x(s)) for s in (1, 2, 3)]
+    core_y0, core_x1 = [], []
+    for other in (2, 1, 3, 0):
+        at_y = (y + other) % 4
+        at_x = (x + other) % 4
+        arrived(core_x0[other])
+        half_x[at_y] = core_sum[x, at_y, low] + core_x[0, at_y] + core_x[1, at_y] + core_x[2, at_y]
+        if other:
+            core_y0.append(send(half_x.at[at_y], end_y.at[other - 1], on_y(other)))
+        arrived(core_y1[other])
+        half_y[at_x] = core_sum[at_x, y, high] + core_y[0, at_x] + core_y[1, at_x] + core_y[2, at_x]
+        if other:
+            core_x1.append(send(half_y.at[at_x], end_x.at[other - 1], on_x(other)))
 
     arrived(rows_s1)
     rows_own = rows_sum[x] + rows_x[0] + rows_x[1] + rows_x[2]
@@ -378,31 +392,52 @@
     turned = jnp.concatenate([tile_all[...], jnp.zeros((64, 128), f32)], axis=0).T
     core_all[c, x, y] = turned[:64] + pltpu.roll(turned[64:], 64, axis=1)
 
-    back_y0 = [send(core_all.at[c, x, y, low], core_all.at[c, x, y, low], on_y(s)) for s in (1, 2, 3)]
-    back_x1 = [send(core_all.at[c, x, y, high], core_all.at[c, x, y, high], on_x(s)) for s in (1, 2, 3)]
-    arrived(back_y0)
-    back_x0 = [send(core_all.at[c, x, :, low], core_all.at[c, x, :, low], on_x(s)) for s in (1, 2, 3)]
-    arrived(back_x1)
-    back_y1 = [send(core_all.at[c, :, y, high], core_all.at[c, :, y, high], on_y(s)) for s in (1, 2, 3)]
+    def pass_low(block_y):
+        block = core_all.at[c, x, block_y, low]
+        return [send(block, block, on_x(s)) for s in far_first]
+
+    def pass_high(block_x):
+        block = core_all.at[c, block_x, y, high]
+        return [send(block, block, on_y(s)) for s in far_first]
+
+    kept, handed = [], []
+
+    def hand(*where):
+        piece, place_out = core_all.at[where], core_out.at[where]
+        handed.append(send(piece, place_out, mate()))
+        kept.append(fetch(piece, place_out, local_sem.at[4 + len(kept)]))
+
+    own_low = core_all.at[c, x, y, low]
+    own_high = core_all.at[c, x, y, high]
+    back_y0 = {s: send(own_low, own_low, on_y(s)) for s in far_first}
+    back_x1 = {s: send(own_high, own_high, on_x(s)) for s in far_first}
+    back_x0 = [pass_low(y)]
+    back_y1 = [pass_high(x)]
+    for s in (1, 3, 2):
+        back_y0[s].wait_recv()
+        back_x0.append(pass_low((y + 4 - s) % 4))
+        back_x1[s].wait_recv()
+        back_y1.append(pass_high((x + 4 - s) % 4))
+    hand(c, x, slice(None), low)
+    hand(c, slice(None), y, high)
 
     arrived(cols_s3)
     whole = cols_all[...].reshape(64, 128)
     cols_out[...] = jnp.where(z % 2 == 1, pltpu.roll(whole, 64, axis=1), whole)[:, :64]
 
-    arrived(back_x0)
-    back_c0 = send(core_all.at[c, :, :, low], core_all.at[c, :, :, low], mate())
-    arrived(back_y1)
-    back_c1 = send(core_all.at[c, :, :, high], core_all.at[c, :, :, high], mate())
+    for place_at, s in ((1, 1), (2, 3), (0, 2)):
+        arrived([blocks[place_at] for blocks in back_x0])
+        hand(c, (x + 4 - s) % 4, slice(None), low)
+        arrived([blocks[place_at] for blocks in back_y1])
+        hand(c, slice(None), (y + 4 - s) % 4, high)
     depth_s4.wait_recv()
     depth_out[...] = depth_all[...].reshape(64, 128)
-    own_half = fetch(core_all.at[c], core_out.at[c], local_sem.at[4])
-    back_c0.wait_recv()
-    back_c1.wait_recv()
-    other_half = fetch(core_all.at[o], core_out.at[o], local_sem.at[5])
+    assert len(started) == send_sem.shape[0] == recv_sem.shape[0]
+    arrived(handed)
+    for copy in kept:
+        copy.wait()
     for copy in started:
         copy.wait_send()
-    own_half.wait()
-    other_half.wait()
 
 
 MIDDLE = 4
@@ -413,7 +448,7 @@
     smem = pl.BlockSpec(memory_space=pltpu.SMEM)
     hbm = pl.BlockSpec(memory_space=pltpu.HBM)
     slots = data.shape[0]
-    copies = 110
+    copies = 142
 
     def buf(*shape):
         return pltpu.VMEM(shape, f32)
@@ -478,7 +513,7 @@
             buf(2, 4, 8, 128),
             pltpu.SemaphoreType.DMA((copies,)),
             pltpu.SemaphoreType.DMA((copies,)),
-            pltpu.SemaphoreType.DMA((6,)),
+            pltpu.SemaphoreType.DMA((12,)),
             pltpu.SemaphoreType.DMA((slots,)),
             pltpu.SemaphoreType.DMA((slots,)),
         ],
@@ -501,7 +536,7 @@
 
 
 def unpack_results(core, rows, cols, depth):
-    steps = 4
+    steps = 2
     part = core.shape[0] // steps
 
     def whole(value):

time: 71.7 us -> 68.5 us (0.955)
  Pallas kernels: 70.2 us -> 67 us
    pallas_call x1, Pallas kernels: 66.4 us -> 64.4 us  [tucker_gradients(): pl.pallas_call(tucker_kernel, out_shape=(jax.ShapeDtypeStruct((2, 4, 4, 6...]
    pallas_call x1, Pallas kernels: 3.82 us -> 2.6 us  [unpack_results(): pl.pallas_call(unpack_kernel, out_shape=(jax.ShapeDtypeStruct((2, 32, 64,...]
where the time goes in v4:
time: 68.5 us; the launch traced here: 68.3 us
  Pallas kernels  67 us (98%)
  between operations  1.29 us (2%)
    pallas_call x1, Pallas kernels, tucker_gradients(): pl.pallas_call(tucker_kernel, out_shape=(jax.ShapeDtypeStruct((2, 4, 4, 6...  64.4 us
    pallas_call x1, Pallas kernels, unpack_results(): pl.pallas_call(unpack_kernel, out_shape=(jax.ShapeDtypeStruct((2, 32, 64,...  2.6 us

profile of v4, /device:TPU:1, one launch (start us, length us, event | category | flops | bytes accessed | tf_op | source)
XLA Modules:
  0.0 68.3 jit_solution(4824366868479344869)
XLA Ops:
  1.3 64.4 %tucker_gradients.1 = (f32[2,4,4,64,128]{4,3,2,1,0:T(8,128)}, f32[16,64]{1,0:T(8,128)}, f32[64,64]{1,0:T(8,128)}, f32[64,128]{1,0:T(8,128)}) custom-call(s32[1,3,1,5]{3,2,1,0:T(1,128)} %bitcast.11, s32[1,1,1]{2,1,0:T(1,128)S(6)} %copy.12.counts, bf16[16,64]{1,0:T(8,128)(2,1)} %bitcast.10, bf16[64,64]{1,0:T(8,128)(2,1)} %cols_hbm.1, ...), custom_call_target="tpu_custom_call" | custom-call | tf_op jit(solution)/shard_map/tucker_gradients/pallas_call | solution.py:459
  65.7 2.6 %unpack_results.1 = (f32[2,32,64,64]{3,2,1,0:T(8,128)}, f32[16,64]{1,0:T(8,128)}, f32[64,64]{1,0:T(8,128)}, f32[64,128]{1,0:T(8,128)}) custom-call(f32[32,64,128]{2,1,0:T(8,128)} %bitcast.9, f32[16,64]{1,0:T(8,128)} %get-tuple-element.13.rows_ref, f32[64,64]{1,0:T(8,128)} %get-tuple-element.14.cols_ref, f32[64,128]{1,0:T(8,128)} %get-tuple-element.15.depth_ref), custom_call_target="tpu_custom_call" | custom-call | tf_op jit(solution)/shard_map/unpack_results/pallas_call | solution.py:545

commit v5 on v4

--- a/solution.py
+++ b/solution.py
@@ -293,20 +293,6 @@
     for group in range(4):
         depth_part = finish_group(c, group, depth_part)
 
-    depth_pieces = []
-    for t in range(4):
-        for half in range(2):
-            piece = jnp.zeros((16, 64), f32)
-            for slot in range(slots):
-                at = half * tall + slot * 16
-                piece = piece + depth_part[at : at + 16] * same(place(slot)[2], t)
-            depth_pieces.append(piece)
-    depth_turned = jnp.concatenate(
-        [jnp.concatenate(depth_pieces, axis=0), jnp.zeros((128, 64), f32)], axis=1
-    ).T[:64]
-    depth_own[...] = depth_turned.reshape(2, 4, 8, 128)
-    depth_c = send(depth_own.at[o], depth_pair, mate())
-
     for group in range(4):
         core_c[group].wait_recv()
         core_sum[group] = core_own[c, group] + core_pair[group]
@@ -321,9 +307,19 @@
         core_y1[other] = [
             send(core_sum.at[at_x, (y + s) % 4, high], core_y.at[s - 1, at_x], on_y(s)) for s in far_first
         ]
-    depth_c.wait_recv()
-    depth_sum[...] = depth_own[c] + depth_pair[...]
-    depth_s1 = [send(depth_sum.at[(x + s) % 4], depth_x.at[s - 1], on_x(s)) for s in (1, 2, 3)]
+    depth_pieces = []
+    for t in range(4):
+        for half in range(2):
+            piece = jnp.zeros((16, 64), f32)
+            for slot in range(slots):
+                at = half * tall + slot * 16
+                piece = piece + depth_part[at : at + 16] * same(place(slot)[2], t)
+            depth_pieces.append(piece)
+    depth_turned = jnp.concatenate(
+        [jnp.concatenate(depth_pieces, axis=0), jnp.zeros((128, 64), f32)], axis=1
+    ).T[:64]
+    depth_own[...] = depth_turned.reshape(2, 4, 8, 128)
+    depth_c = send(depth_own.at[o], depth_pair, mate())
 
     arrived(cols_s1)
     cols_sum[...] = (
@@ -344,6 +340,9 @@
         if other:
             core_x1.append(send(half_y.at[at_x], end_x.at[other - 1], on_x(other)))
 
+    depth_c.wait_recv()
+    depth_sum[...] = depth_own[c] + depth_pair[...]
+    depth_s1 = [send(depth_sum.at[(x + s) % 4], depth_x.at[s - 1], on_x(s)) for s in (1, 2, 3)]
     arrived(rows_s1)
     rows_own = rows_sum[x] + rows_x[0] + rows_x[1] + rows_x[2]
     rows_t[...] = jnp.concatenate([rows_own, jnp.zeros((64, 128), f32)], axis=0).T

time: 68.5 us -> 69 us (level)
  no operation moved by 1% of the time
where the time goes in v5:
time: 69 us; the launch traced here: 68.8 us
  Pallas kernels  67.5 us (98%)
  between operations  1.29 us (2%)
    pallas_call x1, Pallas kernels, tucker_gradients(): pl.pallas_call(tucker_kernel, out_shape=(jax.ShapeDtypeStruct((2, 4, 4, 6...  64.9 us
    pallas_call x1, Pallas kernels, unpack_results(): pl.pallas_call(unpack_kernel, out_shape=(jax.ShapeDtypeStruct((2, 32, 64,...  2.6 us

profile of v5, /device:TPU:1, one launch (start us, length us, event | category | flops | bytes accessed | tf_op | source)
XLA Modules:
  0.0 68.8 jit_solution(15665950142176808489)
XLA Ops:
  1.3 64.9 %tucker_gradients.1 = (f32[2,4,4,64,128]{4,3,2,1,0:T(8,128)}, f32[16,64]{1,0:T(8,128)}, f32[64,64]{1,0:T(8,128)}, f32[64,128]{1,0:T(8,128)}) custom-call(s32[1,3,1,5]{3,2,1,0:T(1,128)} %bitcast.11, s32[1,1,1]{2,1,0:T(1,128)S(6)} %copy.12.counts, bf16[16,64]{1,0:T(8,128)(2,1)} %bitcast.10, bf16[64,64]{1,0:T(8,128)(2,1)} %cols_hbm.1, ...), custom_call_target="tpu_custom_call" | custom-call | tf_op jit(solution)/shard_map/tucker_gradients/pallas_call | solution.py:458
  66.2 2.6 %unpack_results.1 = (f32[2,32,64,64]{3,2,1,0:T(8,128)}, f32[16,64]{1,0:T(8,128)}, f32[64,64]{1,0:T(8,128)}, f32[64,128]{1,0:T(8,128)}) custom-call(f32[32,64,128]{2,1,0:T(8,128)} %bitcast.9, f32[16,64]{1,0:T(8,128)} %get-tuple-element.13.rows_ref, f32[64,64]{1,0:T(8,128)} %get-tuple-element.14.cols_ref, f32[64,128]{1,0:T(8,128)} %get-tuple-element.15.depth_ref), custom_call_target="tpu_custom_call" | custom-call | tf_op jit(solution)/shard_map/unpack_results/pallas_call | solution.py:544
